TPU v7x, 32 devices: a whole 2x2x4 slice. The times are simulated.
32 devices in a mesh: expert: 16 (over z, y, x), tensor: 2 (over core).
Axes of the slice: x: 2, y: 2, z: 4, core: 2. Of those that a mesh axis runs over, the one named last changes fastest.
Arguments:
- moe_in: bfloat16 [4096, 1536], P('expert', 'tensor'), may hold values from -6 to 6
- moe_grad: bfloat16 [4096, 1536], P('expert', 'tensor'), may hold values from -6 to 6
- routes: int32 [4096, 2], P('expert'), may hold values from 0 to 15, all different within a row; in each aligned block of 256 rows (0 to 255, 256 to 511, ...) at most 64 rows name the same one
- gates: float32 [4096, 2], P('expert'), may hold values from 0.25 to 1
- w_in: bfloat16 [16, 1536, 3072], P('expert', None, 'tensor'), may hold values from -0.15625 to 0.15625
- w_out: bfloat16 [16, 3072, 1536], P('expert', 'tensor'), may hold values from -0.109375 to 0.109375
- conv_in: bfloat16 [4096, 1536], P('expert', 'tensor'), may hold values from -6 to 6
- w_glu: bfloat16 [1536, 2, 1536], P(None, None, 'tensor'), may hold values from -0.15625 to 0.15625
- kernel: float32 [32, 1536], P(None, 'tensor'), may hold values from -1 to 1
- conv_grad: bfloat16 [4096, 1536], P('expert', 'tensor'), may hold values from -6 to 6
Outputs:
- moe_input_grad: bfloat16 [1536, 4096], P('tensor', 'expert')
- conv_input_grad: bfloat16 [1536, 4096], P('tensor', 'expert')
Inputs may be any that keep to these rules, and one draw needn't show every extreme that they name: `routes`: each row names two different experts. Among the 256 frames of one index of the expert axis no expert is named by more than 64 of them, a bound that some block reaches.
All inputs are finite; a program needn't handle non-finite values.
Results may differ from a plain program's by a relative error of at most 0.0072.
Values may be sent and summed in bfloat16 or wider, within the bound.
No kernel may reach another device: no remote copies, remote signals or barrier semaphores. Data moves between devices by JAX's collectives and lax.ppermute only.
A program may use at most 128 MiB of HBM per device.

v0:
```python
import jax
import jax.numpy as jnp
from jax import lax
from jax.sharding import PartitionSpec as P


def from_behind(x, axis, by):
    devices = lax.axis_size(axis)
    pairs = [(i, i + by) for i in range(devices) if 0 <= i + by < devices]
    return lax.ppermute(x, axis, pairs)


def body(moe_in, moe_grad, routes, gates, w_in, w_out, conv_in, w_glu, kernel, conv_grad):
    frames = moe_in.shape[0]
    channels = conv_grad.shape[1]
    local = w_in.shape[0]
    sources = lax.axis_size("expert")
    experts = local * sources
    capacity = 4 * frames // experts
    slots = experts * capacity
    pairs = 2 * frames
    model = w_in.shape[1]
    glu_weight = w_glu.reshape(model, 2 * channels)
    flat = routes.reshape(pairs)
    onehot = (flat[:, None] == jnp.arange(experts, dtype=jnp.int32)[None, :]).astype(jnp.int32)
    position = jnp.sum(onehot * jnp.cumsum(onehot, axis=0), axis=1) - 1
    slot = flat * capacity + position
    source = jnp.full((slots,), pairs, jnp.int32).at[slot].set(jnp.arange(pairs, dtype=jnp.int32))
    scaled = (moe_grad.astype(jnp.float32)[:, None, :] * gates[:, :, None]).astype(jnp.bfloat16)
    scaled = jnp.concatenate(
        [scaled.reshape(pairs, channels), jnp.zeros((1, channels), jnp.bfloat16)], axis=0
    )
    padded_in = jnp.concatenate([moe_in, jnp.zeros((1, channels), jnp.bfloat16)], axis=0)
    x_send = padded_in[source // 2]
    g_send = scaled[source]
    x_recv, g_recv = (
        lax.all_to_all(x_send, "expert", split_axis=0, concat_axis=0, tiled=True),
        lax.all_to_all(g_send, "expert", split_axis=0, concat_axis=0, tiled=True),
    )
    pieces = (
        lax.all_gather(x_recv, "tensor", axis=1, tiled=True),
        lax.all_gather(g_recv, "tensor", axis=1, tiled=True),
    )
    width = pieces[0].shape[1]
    x_part = pieces[0].reshape(sources, local, capacity, width)
    g_part = pieces[1].reshape(sources, local, capacity, width)
    first = jnp.einsum("sqcd,qdh->sqch", x_part, w_in, preferred_element_type=jnp.float32)
    second = jnp.einsum("sqcd,qhd->sqch", g_part, w_out, preferred_element_type=jnp.float32)
    rows_glu = glu_weight
    glu_pre = jnp.dot(
        lax.all_gather(conv_in, "tensor", axis=1, tiled=True),
        rows_glu,
        preferred_element_type=jnp.float32,
    )
    sig = jax.nn.sigmoid(first)
    pre_grad = (second * sig * (1.0 + first * (1.0 - sig))).astype(jnp.bfloat16)
    term = jnp.einsum("qih,sqch->isqc", w_in, pre_grad, preferred_element_type=jnp.float32)
    slot_grads = lax.psum_scatter(
        term.reshape(channels * lax.axis_size("tensor"), slots).astype(jnp.bfloat16),
        "tensor",
        scatter_dimension=0,
        tiled=True,
    )
    returned = lax.all_to_all(slot_grads, "expert", split_axis=1, concat_axis=1, tiled=True)
    picked = returned[:, slot].astype(jnp.float32).reshape(channels, frames, 2)
    moe_input_grad = jnp.sum(picked, axis=2).astype(jnp.bfloat16)
    taps = kernel.shape[0]
    future = from_behind(conv_grad[: taps - 1], "expert", -1)
    extended = jnp.concatenate([conv_grad, future], axis=0).astype(jnp.float32)
    mix_grad = jnp.zeros((frames, channels), jnp.float32)
    for offset in range(taps):
        mix_grad = mix_grad + kernel[offset] * extended[offset : offset + frames]
    value = glu_pre[:, :channels]
    gate = glu_pre[:, channels:]
    sig_gate = jax.nn.sigmoid(gate)
    glu_grad = jnp.concatenate(
        [mix_grad * sig_gate, mix_grad * value * sig_gate * (1.0 - sig_gate)], axis=1
    ).astype(jnp.bfloat16)
    rows_glu = glu_weight
    conv_input_grad = lax.psum_scatter(
        lax.dot_general(
            rows_glu, glu_grad, (((1,), (1,)), ((), ())), preferred_element_type=jnp.float32
        ).astype(jnp.bfloat16),
        "tensor",
        scatter_dimension=0,
        tiled=True,
    )
    return (moe_input_grad, conv_input_grad)


def solution(mesh):
    placed = (
        P("expert", "tensor"),
        P("expert", "tensor"),
        P("expert", None),
        P("expert", None),
        P("expert", None, "tensor"),
        P("expert", "tensor", None),
        P("expert", "tensor"),
        P(None, None, "tensor"),
        P(None, "tensor"),
        P("expert", "tensor"),
    )
    return jax.shard_map(
        body,
        mesh=mesh,
        in_specs=placed,
        out_specs=(P("tensor", "expert"), P("tensor", "expert")),
        check_vma=False,
    )
```

profile of v0, /device:TPU:12, one launch (start us, length us, event | category | flops | bytes accessed | tf_op | source)
XLA Modules:
  0.0 207.2 jit_solution(6990360619382237161)
XLA Ops:
  7.2 0.7 broadcast_multiply_fusion
  7.8 0.8 copy.21
  8.7 0.1 eq.25
  8.8 0.1 eq.29
  9.0 0.1 copy.20
  9.1 0.1 mul.385
  9.3 1.2 reduce-window.6
  10.4 0.2 slice_reduce_fusion
  10.7 0.1 fusion.62
  10.8 2.4 %scatter_custom_fusion = s32[1024]{0:T(1024)S(1)} fusion(s32[512]{0:T(512)S(1)} %bitcast.104, s32[512]{0:T(512)S(1)} %iota.11, s32[]{:T(128)} %constant.14.clone.1), kind=kCustom, calls=%fused_computation.153 | custom fusion | bytes 4100 | tf_op jit(solution)/shard_map/scatter | solution.py:28
  13.3 1.0 concatenate.14
  14.3 5.2 %gather_fusion.1 = bf16[1024,768]{1,0:T(8,128)(2,1)} fusion(bf16[257,768]{1,0:T(8,128)(2,1)S(1)} %concatenate.14, s32[1024]{0:T(1024)S(1)} %get-tuple-element.43), kind=kCustom, calls=%fused_computation.1 | custom fusion | bytes 3149824 | tf_op jit(solution)/shard_map/gather | solution.py:34
  19.5 7.3 %all-to-all-start.1 = ((bf16[16,64,768]{2,1,0:T(8,128)(2,1)}), bf16[16,64,768]{2,1,0:T(8,128)(2,1)S(1)}, u32[]{:S(2)}, u32[]{:S(2)}) async-start(bf16[16,64,768]{2,1,0:T(8,128)(2,1)} %bitcast.11), calls=%async_computation.1 | async-start | bytes 3145728 | tf_op jit(solution)/shard_map/all_to_all | solution.py:37
  26.9 1.6 mul.378
  28.4 2.4 %mul.379 = f32[512,768]{1,0:T(8,128)S(1)} reshape(f32[256,2,768]{2,1,0:T(2,128)} %mul.378) | data formatting | bytes 3145728 | tf_op jit(solution)/shard_map/mul | solution.py:29
  30.8 0.1 copy.19
  31.0 0.1 mul.380
  31.1 32.9 %all-to-all-done.1 = bf16[16,64,768]{2,1,0:T(8,128)(2,1)S(1)} async-done(((bf16[16,64,768]{2,1,0:T(8,128)(2,1)}), bf16[16,64,768]{2,1,0:T(8,128)(2,1)S(1)}, u32[]{:S(2)}, u32[]{:S(2)}) %all-to-all-start.1) | async-done | bytes 1572896 | tf_op jit(solution)/shard_map/all_to_all | solution.py:37
  64.0 1.2 copy-done
  65.2 0.0 all-gather.3.cloned.1.call-start
  65.2 0.1 multiply_convert_fusion
  65.4 0.1 concatenate.13
  65.4 4.0 %gather_fusion = bf16[1024,768]{1,0:T(8,128)(2,1)S(1)} fusion(bf16[513,768]{1,0:T(8,128)(2,1)S(1)} %concatenate.13, s32[1024]{0:T(1024)S(1)} %get-tuple-element.42), kind=kCustom, calls=%fused_computation | custom fusion | bytes 3149824 | tf_op jit(solution)/shard_map/gather | solution.py:35
  69.4 40.3 %all_to_all.36 = bf16[16,64,768]{2,1,0:T(8,128)(2,1)} all-to-all(bf16[16,64,768]{2,1,0:T(8,128)(2,1)S(1)} %bitcast.97), channel_id=1, replica_groups=mesh['expert'=16,'tensor'=2] {'expert'}, dimensions={0} | all-to-all | bytes 3145728 | tf_op jit(solution)/shard_map/all_to_all | solution.py:38
  109.7 0.0 reduce-scatter.3.cloned.1.call-start
  109.8 9.8 %fusion.8 = f32[16,64,1536]{2,1,0:T(8,128)} fusion(bf16[16,64,1536]{2,1,0:T(8,128)(2,1)} %bitcast.109, bf16[1,1536,1536]{2,1,0:T(8,128)(2,1)} %param.14), kind=kOutput, calls=%fused_computation.15 | convolution fusion | flops 4831838208 | bytes 14155776 | tf_op jit(solution)/shard_map/sqcd,qdh->sqch/dot_general | solution.py:47
  119.6 1.8 all-gather.3.cloned.1.call-done
  121.4 10.2 %fusion.17 = bf16[16,64,1536]{2,1,0:T(8,128)(2,1)S(1)} fusion(f32[16,64,1536]{2,1,0:T(8,128)} %fusion.8, bf16[16,64,1536]{2,1,0:T(8,128)(2,1)} %bitcast.110, bf16[1,1536,1536]{2,1,0:T(8,128)(2,1)} %param.15), kind=kOutput, calls=%fused_computation.20 | convolution fusion | flops 4845993984 | bytes 17301504 | tf_op jit(solution)/shard_map/sqcd,qhd->sqch/dot_general | solution.py:48
  131.6 6.5 %fusion.14 = bf16[16,64,1536]{2,1,0:T(8,128)(2,1)} fusion(bf16[16,64,1536]{2,1,0:T(8,128)(2,1)S(1)} %fusion.17, bf16[1,1536,1536]{2,1,0:T(8,128)(2,1)S(1)} %bitcast.108), kind=kOutput, calls=%fused_computation.19 | convolution fusion | flops 4833411072 | bytes 11010048 | tf_op jit(solution)/shard_map/qih,sqch->isqc/dot_general | solution.py:57
  138.1 1.0 copy-done.3
  139.1 3.4 %collective-permute-start = (bf16[31,768]{1,0:T(8,128)(2,1)S(1)}, bf16[31,768]{1,0:T(8,128)(2,1)S(1)}, u32[]{:S(2)}, u32[]{:S(2)}) collective-permute-start(bf16[31,768]{1,0:T(8,128)(2,1)S(1)} %slice.210), channel_id=1, source_target_pairs={{2,0},{4,2},{6,4},{8,6},{10,8},{12,10},{14,12},{16,14},{18,16},{20... | collective-permute-start | bytes 142856 | tf_op jit(solution)/shard_map/ppermute | solution.py:10
  142.5 3.3 %copy.27 = bf16[192,8,2,768]{3,1,2,0:T(8,128)(2,1)S(1)} copy(bf16[192,8,2,768]{3,2,1,0:T(2,128)(2,1)} %bitcast.98) | data formatting | bytes 9437184
  145.8 0.2 slice_reduce_fusion.32
  146.0 2.5 %all_gather.11 = bf16[256,1536]{1,0:T(8,128)(2,1)S(1)} all-gather(bf16[256,768]{1,0:T(8,128)(2,1)S(1)} %copy-done.4), channel_id=1, replica_groups=mesh['expert'=16,'tensor'=2] {'tensor'}, dimensions={1}, use_global_device_ids=true | all-gather | bytes 1179648 | tf_op jit(solution)/shard_map/all_gather | solution.py:51
  148.5 2.6 %fusion.72 = f32[256,1536]{1,0:T(8,128)} fusion(bf16[256,1536]{1,0:T(8,128)(2,1)S(1)} %all_gather.11, bf16[1536,1536]{1,0:T(8,128)(2,1)S(1)} %bitcast.99), kind=kOutput, calls=%fused_computation.158 | convolution fusion | flops 1207959552 | bytes 7077888 | tf_op jit(solution)/shard_map/dot_general | solution.py:50
  151.1 0.1 slice_reduce_fusion.31
  151.2 0.1 maximum_convert_fusion
  151.3 6.6 %all-to-all-start.2 = ((bf16[768,16,64]{0,2,1:T(8,128)(2,1)}), bf16[768,16,64]{0,2,1:T(8,128)(2,1)S(1)}, u32[]{:S(2)}, u32[]{:S(2)}) async-start(bf16[768,16,64]{0,2,1:T(8,128)(2,1)} %bitcast.103), calls=%async_computation.3 | async-start | bytes 3145728 | tf_op jit(solution)/shard_map/all_to_all | solution.py:64
  158.0 4.4 %multiply_convert_fusion.1 = (bf16[256,768]{1,0:T(8,128)(2,1)S(1)}, f32[256,768]{1,0:T(8,128)S(1)}) fusion(f32[256,1536]{1,0:T(8,128)} %fusion.72, f32[287,768]{1,0:T(8,128)S(1)} %maximum_convert_fusion, f32[768]{0:T(1024)S(1)} %get-tuple-element.38, f32[768]{0:T(1024)S(1)} %get-tuple-element.39, f32[768]{0:T(1024)S(1)} %get-tuple-element.9, ...), kind=kLoop, calls=%fused_computation.98 | loop fusion | flops 13369344 | bytes 27230208 | tf_op jit(solution)/shard_map/convert.1
  162.5 0.2 fusion.23
  162.7 4.6 %fusion.20 = bf16[1536,256]{0,1:T(8,128)(2,1)} fusion(bf16[1536,1536]{1,0:T(8,128)(2,1)} %bitcast.100, bf16[256,768]{1,0:T(8,128)(2,1)S(1)} %fusion.23, bf16[256,768]{1,0:T(8,128)(2,1)S(1)} %get-tuple-element.40), kind=kOutput, calls=%fused_computation.22 | convolution fusion | flops 1209925632 | bytes 6291456 | tf_op jit(solution)/shard_map/dot_general | solution.py:81
  167.4 9.4 %reduce-scatter.5.cloned.1.call-done = bf16[768,256]{0,1:T(8,128)(2,1)} async-done(((bf16[1536,256]{0,1:T(8,128)(2,1)}), bf16[768,256]{0,1:T(8,128)(2,1)}) %reduce-scatter.5.cloned.1.call-update) | async-done | bytes 393232 | tf_op jit(solution)/shard_map/reduce_scatter | solution.py:80
  176.8 1.9 copy.25
  178.7 16.6 %all-to-all-done.2 = bf16[768,16,64]{0,2,1:T(8,128)(2,1)S(1)} async-done(((bf16[768,16,64]{0,2,1:T(8,128)(2,1)}), bf16[768,16,64]{0,2,1:T(8,128)(2,1)S(1)}, u32[]{:S(2)}, u32[]{:S(2)}) %all-to-all-start.2) | async-done | bytes 1572896 | tf_op jit(solution)/shard_map/all_to_all | solution.py:64
  195.3 2.0 gather_fusion.2
  197.3 0.3 gather.14
  197.6 2.1 %reduce_sum.22 = bf16[768,256]{0,1:T(8,128)(2,1)S(1)} reduce(bf16[768,256,2]{0,2,1:T(2,128)(2,1)S(1)} %gather.14, bf16[]{:T(256)} %constant.13.clone.1), dimensions={2}, to_apply=%region_5.6 | reduce | flops 196608 | bytes 1179650 | tf_op jit(solution)/shard_map/reduce_sum | solution.py:66
  199.7 0.9 copy.24
  (37 shorter events, 0.3 us)
Async XLA Ops:
  19.5 7.4 %copy-start.5 = (bf16[256,768]{1,0:T(8,128)(2,1)S(1)}, bf16[256,768]{1,0:T(8,128)(2,1)}, u32[]{:S(2)}) copy-start(bf16[256,768]{1,0:T(8,128)(2,1)} %param.11) | copy-start | bytes 1179652
  19.5 44.5 %all-to-all-start.1 = ((bf16[16,64,768]{2,1,0:T(8,128)(2,1)}), bf16[16,64,768]{2,1,0:T(8,128)(2,1)S(1)}, u32[]{:S(2)}, u32[]{:S(2)}) async-start(bf16[16,64,768]{2,1,0:T(8,128)(2,1)} %bitcast.11), calls=%async_computation.1 | async-start | bytes 3145728 | tf_op jit(solution)/shard_map/all_to_all | solution.py:37
  26.8 4.0 %copy-start.7 = (f32[256,2]{0,1:T(2,128)S(1)}, f32[256,2]{0,1:T(2,128)}, u32[]{:S(2)}) copy-start(f32[256,2]{0,1:T(2,128)} %param.13) | copy-start | bytes 6148
  26.8 83.0 %all-gather.5.cloned.1.call-start = ((), (), s32[]{:S(2)}) async-start(), calls=%async_computation.6 | async-start | bytes 4718592 | tf_op jit(solution)/shard_map/all_gather | solution.py:41
  64.0 1.2 copy-start
  65.2 56.2 %all-gather.3.cloned.1.call-start = ((), (), s32[]{:S(2)}) async-start(), calls=%async_computation.5 | async-start | bytes 4718592 | tf_op jit(solution)/shard_map/all_gather | solution.py:42
  109.7 41.6 %reduce-scatter.3.cloned.1.call-start = ((), (), s32[]{:S(2)}) async-start(), calls=%async_computation.7 | async-start | bytes 4718592 | tf_op jit(solution)/shard_map/reduce_scatter | solution.py:58
  109.8 21.8 %slice-start = ((s8[4718592]{0:T(1024)(128)(4,1)}), s8[524288]{0:T(1024)(128)(4,1)S(1)}, s32[]{:S(2)}) async-start(s8[4718592]{0:T(1024)(128)(4,1)} %bitcast.107), calls=%async_computation.9 | async-start | bytes 1048576
  121.4 10.2 %slice-start.1 = ((s8[4718592]{0:T(1024)(128)(4,1)}), s8[4194304]{0:T(1024)(128)(4,1)S(1)}, s32[]{:S(2)}) async-start(s8[4718592]{0:T(1024)(128)(4,1)} %bitcast.107), calls=%async_computation.10 | async-start | bytes 8388608
  138.1 1.0 copy-start.3
  139.1 12.1 %collective-permute-start = (bf16[31,768]{1,0:T(8,128)(2,1)S(1)}, bf16[31,768]{1,0:T(8,128)(2,1)S(1)}, u32[]{:S(2)}, u32[]{:S(2)}) collective-permute-start(bf16[31,768]{1,0:T(8,128)(2,1)S(1)} %slice.210), channel_id=1, source_target_pairs={{2,0},{4,2},{6,4},{8,6},{10,8},{12,10},{14,12},{16,14},{18,16},{20... | collective-permute-start | bytes 142856 | tf_op jit(solution)/shard_map/ppermute | solution.py:10
  142.4 3.4 %copy-start.6 = (f32[32,768]{1,0:T(8,128)S(1)}, f32[32,768]{1,0:T(8,128)}, u32[]{:S(2)}) copy-start(f32[32,768]{1,0:T(8,128)} %param.18) | copy-start | bytes 294916
  142.5 3.5 %copy-start.4 = (bf16[256,768]{1,0:T(8,128)(2,1)S(1)}, bf16[256,768]{1,0:T(8,128)(2,1)}, u32[]{:S(2)}) copy-start(bf16[256,768]{1,0:T(8,128)(2,1)} %param.16) | copy-start | bytes 1179652
  145.8 5.3 %copy-start.1 = (bf16[192,8,2,768]{3,1,2,0:T(8,128)(2,1)}, bf16[192,8,2,768]{3,1,2,0:T(8,128)(2,1)S(1)}, u32[]{:S(2)}) copy-start(bf16[192,8,2,768]{3,1,2,0:T(8,128)(2,1)S(1)} %copy.27) | copy-start | bytes 14155780
  151.3 44.0 %all-to-all-start.2 = ((bf16[768,16,64]{0,2,1:T(8,128)(2,1)}), bf16[768,16,64]{0,2,1:T(8,128)(2,1)S(1)}, u32[]{:S(2)}, u32[]{:S(2)}) async-start(bf16[768,16,64]{0,2,1:T(8,128)(2,1)} %bitcast.103), calls=%async_computation.3 | async-start | bytes 3145728 | tf_op jit(solution)/shard_map/all_to_all | solution.py:64
  158.0 18.8 %reduce-scatter.5.cloned.1.call-start = ((), (), s32[]{:S(2)}) async-start(), calls=%async_computation.8 | async-start | bytes 1179648 | tf_op jit(solution)/shard_map/reduce_scatter | solution.py:80
  158.0 4.5 %copy-start.2 = (f32[256,1536]{1,0:T(8,128)S(1)}, f32[256,1536]{1,0:T(8,128)}, u32[]{:S(2)}) copy-start(f32[256,1536]{1,0:T(8,128)} %fusion.72) | copy-start | bytes 4718596
Sparse Core Ops, SparseCore 0:
  65.3 11.0 all-gather.4
  109.8 11.4 all-gather.2
  138.2 12.2 reduce-scatter.2
  167.5 9.2 reduce-scatter.4
where the time goes:
time: 208 us; the launch traced here: 207 us
  waiting for transfers between devices  60.7 us (29%)
  blocking collectives  42.8 us (21%)
  matrix products  33.6 us (16%)
  local copies, waits for them, and re-layouts  29.4 us (14%)
  starting transfers between devices  17.5 us (8%)
  between operations  14.1 us (7%)
  other arithmetic  9.01 us (4%)
    all_to_all x1, blocking collectives, body(): lax.all_to_all(g_send, 'expert', split_axis=0, concat_axis=0, tiled=True)  40.3 us
    all_to_all x1, waiting for transfers between devices, body(): lax.all_to_all(x_send, 'expert', split_axis=0, concat_axis=0, tiled=True)  32.9 us
    all_to_all x1, waiting for transfers between devices, body(): lax.all_to_all(slot_grads, 'expert', split_axis=1, concat_axis=1, tiled=T...  16.6 us
    dot_general x1, matrix products, body(): jnp.einsum('sqcd,qhd->sqch', g_part, w_out, preferred_element_type=jnp.fl...  10.2 us
    dot_general x1, matrix products, body(): jnp.einsum('sqcd,qdh->sqch', x_part, w_in, preferred_element_type=jnp.flo...  9.77 us
    reduce_scatter x1, waiting for transfers between devices, body(): lax.psum_scatter(lax.dot_general(rows_glu, glu_grad, (((1,), (1,)), ((),...  9.37 us
    unnamed x25, local copies, waits for them, and re-layouts  9.26 us
    all_to_all x1, starting transfers between devices, body(): lax.all_to_all(x_send, 'expert', split_axis=0, concat_axis=0, tiled=True)  7.3 us
  transfers between devices with their start and end apart: 7, of which 4 were waited for; matrix products, arithmetic and copies ran while one was open for 17% of the time, Pallas kernels for 0%

commit v1 on v0

v1 whole, which is shorter than its diff:
```python
import jax
import jax.numpy as jnp
from jax import lax
from jax.experimental import pallas as pl
from jax.experimental.pallas import tpu as pltpu
from jax.sharding import PartitionSpec as P

BF = jnp.bfloat16
F32 = jnp.float32


def swap(x):
    return lax.ppermute(x, "tensor", [(0, 1), (1, 0)])


def gather_channels(x):
    if lax.axis_size("tensor") != 2:
        return lax.all_gather(x, "tensor", axis=1, tiled=True)
    other = swap(x)
    first = lax.axis_index("tensor") == 0
    return jnp.concatenate([jnp.where(first, x, other), jnp.where(first, other, x)], axis=1)


def scatter_sum(term, axis):
    if lax.axis_size("tensor") != 2:
        return lax.psum_scatter(term, "tensor", scatter_dimension=axis, tiled=True)
    first = lax.axis_index("tensor") == 0
    low, high = jnp.split(term, 2, axis=axis)
    other = swap(jnp.where(first, high, low))
    own = jnp.where(first, low, high)
    return (own.astype(F32) + other.astype(F32)).astype(BF)


def slot_of(routes_t, frames, first, number):
    experts = first + lax.broadcasted_iota(jnp.int32, (number, frames), 0)
    named = (routes_t[0:1] == experts) | (routes_t[1:2] == experts)
    before = lax.broadcasted_iota(jnp.int32, (frames, frames), 0) < lax.broadcasted_iota(
        jnp.int32, (frames, frames), 1
    )
    count = jnp.dot(named.astype(BF), before.astype(BF), preferred_element_type=F32)
    return jnp.where(named, count.astype(jnp.int32), -1), experts


def one_hot(slot, capacity):
    number, frames = slot.shape
    place = lax.broadcasted_iota(jnp.int32, (number, capacity, frames), 1)
    return (slot[:, None, :] == place).reshape(number * capacity, frames)


def dispatch_kernel(base_ref, r_ref, g_ref, in_ref, grad_ref, out_ref):
    number, twice, channels = out_ref.shape
    capacity = twice // 2
    frames = r_ref.shape[1]
    experts = base_ref[0] + lax.broadcasted_iota(jnp.int32, (number, frames), 0)
    one = r_ref[0:1, :] == experts
    two = r_ref[1:2, :] == experts
    named = jnp.where(one, 1.0, jnp.where(two, 1.0, 0.0))
    before = lax.broadcasted_iota(jnp.int32, (frames, frames), 0) < lax.broadcasted_iota(
        jnp.int32, (frames, frames), 1
    )
    count = jnp.dot(named.astype(BF), jnp.where(before, 1.0, 0.0).astype(BF), preferred_element_type=F32)
    slot = jnp.where(named > 0.0, count.astype(jnp.int32), -1)
    gate = jnp.where(one, g_ref[0:1, :], g_ref[1:2, :])
    place = lax.broadcasted_iota(jnp.int32, (number, capacity, frames), 1)
    hot = jnp.broadcast_to(slot[:, None, :], place.shape) == place
    scale = jnp.sum(jnp.where(hot, jnp.broadcast_to(gate[:, None, :], place.shape), 0.0), axis=2, keepdims=True)
    hot = jnp.where(hot, 1.0, 0.0).reshape(number * capacity, frames).astype(BF)
    x = jnp.dot(hot, in_ref[...], preferred_element_type=F32).astype(BF)
    g = jnp.dot(hot, grad_ref[...], preferred_element_type=F32).reshape(number, capacity, channels) * scale
    out_ref[:, :capacity, :] = x.reshape(number, capacity, channels)
    out_ref[:, capacity:, :] = g.astype(BF)


def dispatch(base, number, capacity, r, g, in_rows, grad_rows):
    frames, channels = in_rows.shape
    vmem = pl.BlockSpec(memory_space=pltpu.VMEM)
    flops = 4 * number * capacity * frames * channels
    return pl.pallas_call(
        dispatch_kernel,
        out_shape=jax.ShapeDtypeStruct((number, 2 * capacity, channels), BF),
        in_specs=[pl.BlockSpec(memory_space=pltpu.SMEM)] + [vmem] * 4,
        out_specs=vmem,
        cost_estimate=pl.CostEstimate(
            flops=flops, bytes_accessed=4 * channels * (frames + number * capacity), transcendentals=0
        ),
        compiler_params=pltpu.CompilerParams(vmem_limit_bytes=16 << 20),
        name="dispatch",
    )(base.reshape(1), r, g, in_rows, grad_rows)


def finish_kernel(place_ref, here_ref, back_ref, *rest):
    rest[-1][...] = (here_ref[...].astype(F32) + back_ref[...].astype(F32)).astype(BF)


def finish(place, here, back, others):
    rows, channels = here.shape
    extra = [] if others is None else [others]
    steps = 2
    return pl.pallas_call(
        finish_kernel,
        out_shape=jax.ShapeDtypeStruct((2 * rows, channels), BF),
        grid_spec=pltpu.PrefetchScalarGridSpec(
            num_scalar_prefetch=1,
            grid=(steps,),
            in_specs=[pl.BlockSpec((rows // steps, channels), lambda i, place: (i, 0))] * 2
            + [pl.BlockSpec(memory_space=pl.ANY)] * len(extra),
            out_specs=pl.BlockSpec((rows // steps, channels), lambda i, place: (place[0] * steps + i, 0)),
        ),
        input_output_aliases={3: 0} if extra else {},
        cost_estimate=pl.CostEstimate(
            flops=rows * channels, bytes_accessed=6 * rows * channels, transcendentals=0
        ),
        compiler_params=pltpu.CompilerParams(vmem_limit_bytes=8 << 20),
        name="finish",
    )(place.reshape(1), here, back, *extra)


def body(moe_in, moe_grad, routes, gates, w_in, w_out, conv_in, w_glu, kernel, conv_grad):
    frames, channels = moe_in.shape
    sources = lax.axis_size("expert")
    half = sources // 2
    capacity = 4 * frames // sources
    rows = half * capacity
    model = w_in.shape[1]
    w_in, w_out = w_in[0], w_out[0]
    me = lax.axis_index("expert")
    base = me & half
    halves = [list(range(half)), list(range(half, sources))]
    mirror = [(i, i ^ half) for i in range(sources)]

    def in_half(rows):
        return lax.all_to_all(
            rows, "expert", split_axis=0, concat_axis=0, tiled=True, axis_index_groups=halves
        )

    far_routes = lax.ppermute(routes, "expert", mirror).T
    far_gates = lax.ppermute(gates, "expert", mirror).T
    routes_t, gates_t = routes.T, gates.T
    far_in = lax.ppermute(moe_in, "expert", mirror)
    far_grad = lax.ppermute(moe_grad, "expert", mirror)

    both = dispatch(base, half, capacity, routes_t, gates_t, moe_in, moe_grad)
    near_rows = in_half(both).reshape(half, 2, capacity, channels)
    both = dispatch(base, half, capacity, far_routes, far_gates, far_in, far_grad)
    far_rows = in_half(both).reshape(half, 2, capacity, channels)

    def hidden(first, second):
        sig = jax.nn.sigmoid(first)
        return (second * sig * (1.0 + first * (1.0 - sig))).astype(BF)

    def times(a, w, over):
        return lax.dot_general(a, w, (((1,), (over,)), ((), ())), preferred_element_type=F32)

    if lax.axis_size("tensor") == 2:
        core = lax.axis_index("tensor")
        own, oth = core * channels, (1 - core) * channels
        in_own = lax.dynamic_slice_in_dim(w_in, own, channels, 0)
        in_oth = lax.dynamic_slice_in_dim(w_in, oth, channels, 0)
        out_own = lax.dynamic_slice_in_dim(w_out, own, channels, 1)
        out_oth = lax.dynamic_slice_in_dim(w_out, oth, channels, 1)

    near_at = base // half

    def expert(pairs, place, others):
        if lax.axis_size("tensor") != 2:
            x = gather_channels(pairs[:, 0].reshape(rows, channels))
            g = gather_channels(pairs[:, 1].reshape(rows, channels))
            pre_grad = hidden(times(x, w_in, 0), times(g, w_out, 1))
            part = scatter_sum(times(pre_grad, w_in, 1).astype(BF), 1)
            others = jnp.zeros((2 * rows, channels), BF) if others is None else others
            return lax.dynamic_update_slice_in_dim(others, part, place * rows, 0)
        other = swap(pairs)
        first = times(pairs[:, 0].reshape(rows, channels), in_own, 0)
        second = times(pairs[:, 1].reshape(rows, channels), out_own, 1)
        first = first + times(other[:, 0].reshape(rows, channels), in_oth, 0)
        second = second + times(other[:, 1].reshape(rows, channels), out_oth, 1)
        pre_grad = hidden(first, second)
        away = times(pre_grad, in_oth, 1).astype(BF)
        back = swap(away)
        here = times(pre_grad, in_own, 1).astype(BF)
        return finish(place, here, back, others)

    slot_grads = expert(near_rows, near_at, None)
    slot_grads = expert(far_rows, 1 - near_at, slot_grads)

    returned = lax.all_to_all(
        slot_grads.reshape(sources, capacity, channels), "expert", split_axis=0, concat_axis=0, tiled=True
    ).reshape(sources * capacity, channels)
    slot_all, _ = slot_of(routes_t, frames, 0, sources)
    hot_all = one_hot(slot_all, capacity)
    moe_input_grad = lax.dot_general(
        returned, hot_all.astype(BF), (((0,), (0,)), ((), ())), preferred_element_type=F32
    ).astype(BF)

    conv_wide = gather_channels(conv_in)
    glu_weight = w_glu.reshape(model, 2 * channels)
    glu_pre = jnp.dot(conv_wide, glu_weight, preferred_element_type=F32)
    taps = kernel.shape[0]
    future = lax.ppermute(conv_grad[: taps - 1], "expert", [(i, i - 1) for i in range(1, sources)])
    extended = jnp.concatenate([conv_grad, future], axis=0).astype(F32)
    mix_grad = jnp.zeros((frames, channels), F32)
    for offset in range(taps):
        mix_grad = mix_grad + kernel[offset] * extended[offset : offset + frames]
    value = glu_pre[:, :channels]
    gate = glu_pre[:, channels:]
    sig_gate = jax.nn.sigmoid(gate)
    glu_grad = jnp.concatenate([mix_grad * sig_gate, mix_grad * value * sig_gate * (1.0 - sig_gate)], axis=1).astype(BF)
    term = lax.dot_general(
        glu_weight, glu_grad, (((1,), (1,)), ((), ())), preferred_element_type=F32
    ).astype(BF)
    conv_input_grad = scatter_sum(term, 0)
    return (moe_input_grad, conv_input_grad)


def solution(mesh):
    placed = (
        P("expert", "tensor"),
        P("expert", "tensor"),
        P("expert", None),
        P("expert", None),
        P("expert", None, "tensor"),
        P("expert", "tensor", None),
        P("expert", "tensor"),
        P(None, None, "tensor"),
        P(None, "tensor"),
        P("expert", "tensor"),
    )

    return jax.shard_map(
        body,
        mesh=mesh,
        in_specs=placed,
        out_specs=(P("tensor", "expert"), P("tensor", "expert")),
        check_vma=False,
    )
```

time: 208 us -> 159 us (0.76)
  blocking collectives: 42.8 us -> 0 us
  local copies, waits for them, and re-layouts: 29.4 us -> 15.2 us
  between operations: 14.1 us -> 1.06 us
  starting transfers between devices: 17.5 us -> 27.6 us
  waiting for transfers between devices: 60.7 us -> 67.3 us
  Pallas kernels: 0 us -> 5.94 us
  other arithmetic: 9.01 us -> 5.61 us
    ppermute x1 -> x11, waiting for transfers between devices: 0.01 us -> 41.9 us  [the longest x1 30.8 us: body(): far_routes = lax.ppermute(routes, 'expert', mirror).T]
    all_to_all x1 -> x0, blocking collectives: 40.3 us -> none  [body(): lax.all_to_all(g_send, 'expert', split_axis=0, concat_axis=0, tiled=True)]
    all_to_all x2 -> x3, waiting for transfers between devices: 49.5 us -> 25.5 us  [the longest x1 25.4 us: body(): lax.all_to_all(slot_grads.reshape(sources, capacity, channels), 'expert',...]
    gather x4 -> x0, local copies, waits for them, and re-layouts: 11.5 us -> none  [the longest x1 5.21 us: body(): x_send = padded_in[source // 2]]
    reduce_scatter x2 -> x0, waiting for transfers between devices: 9.39 us -> none  [the longest x1 9.37 us: body(): lax.psum_scatter(lax.dot_general(rows_glu, glu_grad, (((1,), (1,)), ((),...]
    ppermute x1 -> x11, starting transfers between devices: 3.35 us -> 10.5 us  [the longest x1 3.37 us: body(): lax.ppermute(conv_grad[:taps - 1], 'expert', [(i, i - 1) for i in range(1...]
    pallas_call x0 -> x4, Pallas kernels: none -> 5.94 us  [the longest x2 3.88 us: dispatch(): pl.pallas_call(dispatch_kernel, out_shape=jax.ShapeDtypeStruct((number, 2...]
    mul x5 -> x0, local copies, waits for them, and re-layouts: 4.34 us -> none  [the longest x3 4.06 us: body(): moe_grad.astype(jnp.float32)[:, None, :] * gates[:, :, None]]
  transfers between devices with their start and end apart: 7 -> 14, of which waited for: 4 -> 4; matrix products, arithmetic and copies ran while one was open for 17% -> 31% of each run, Pallas kernels for 0% -> 2%
where the time goes in v1:
time: 159 us; the launch traced here: 158 us
  waiting for transfers between devices  67.3 us (42%)
  matrix products  35.3 us (22%)
  starting transfers between devices  27.6 us (17%)
  local copies, waits for them, and re-layouts  15.2 us (10%)
  Pallas kernels  5.94 us (4%)
  other arithmetic  5.61 us (4%)
    ppermute x1, waiting for transfers between devices, body(): far_routes = lax.ppermute(routes, 'expert', mirror).T  30.8 us
    dot_general x12, matrix products, times(): lax.dot_general(a, w, (((1,), (over,)), ((), ())), preferred_element_type...  28.5 us
    all_to_all x1, waiting for transfers between devices, body(): lax.all_to_all(slot_grads.reshape(sources, capacity, channels), 'expert',...  25.4 us
    unnamed x42, local copies, waits for them, and re-layouts  11.5 us
    all_to_all x2, starting transfers between devices, in_half(): lax.all_to_all(rows, 'expert', split_axis=0, concat_axis=0, tiled=True, a...  11.4 us
    ppermute x1, waiting for transfers between devices, body(): lax.ppermute(conv_grad[:taps - 1], 'expert', [(i, i - 1) for i in range(1...  9.48 us
    all_to_all x1, starting transfers between devices, body(): lax.all_to_all(slot_grads.reshape(sources, capacity, channels), 'expert',...  5.63 us
    pallas_call x2, Pallas kernels, dispatch(): pl.pallas_call(dispatch_kernel, out_shape=jax.ShapeDtypeStruct((number, 2...  3.88 us
  transfers between devices with their start and end apart: 14, of which 4 were waited for; matrix products, arithmetic and copies ran while one was open for 31% of the time, Pallas kernels for 2%

profile of v1, /device:TPU:12, one launch (start us, length us, event | category | flops | bytes accessed | tf_op | source)
XLA Modules:
  0.0 158.0 jit_solution(321510288291678995)
XLA Ops:
  0.7 1.0 copy-done
  1.7 1.0 copy-done.2
  2.7 0.7 copy-done.4
  3.3 0.7 copy-done.6
  4.0 1.9 %dispatch.3 = bf16[8,128,768]{2,1,0:T(8,128)(2,1)} custom-call(s32[1]{0:T(128)} %bitcast.1.base_ref, s32[2,256]{1,0:T(2,128)S(1)} %bitcast.79, f32[2,256]{1,0:T(2,128)S(1)} %bitcast.81, bf16[256,768]{1,0:T(8,128)(2,1)S(1)} %copy-done, bf16[256,768]{1,0:T(8,128)(2,1)S(1)} %copy-done.2), custom_call_target="tpu_custom_call" | custom-call | flops 402653184 | bytes 2359296 | tf_op jit(solution)/shard_map/dispatch/pallas_call | solution.py:78
  5.9 5.1 %all-to-all-start.1 = ((bf16[8,128,768]{2,1,0:T(8,128)(2,1)}), bf16[8,128,768]{2,1,0:T(8,128)(2,1)S(1)}, u32[]{:S(2)}, u32[]{:S(2)}) async-start(bf16[8,128,768]{2,1,0:T(8,128)(2,1)} %dispatch.3), calls=%async_computation.1 | async-start | bytes 3145728 | tf_op jit(solution)/shard_map/all_to_all | solution.py:132
  11.1 2.7 %collective-permute-start.2 = (bf16[256,768]{1,0:T(8,128)(2,1)S(1)}, bf16[256,768]{1,0:T(8,128)(2,1)S(1)}, u32[]{:S(2)}, u32[]{:S(2)}) collective-permute-start(bf16[256,768]{1,0:T(8,128)(2,1)S(1)} %copy-done.1), channel_id=1, source_target_pairs={{0,16},{2,18},{4,20},{6,22},{8,24},{10,26},{12,28},{14,30},{16,0},... | collective-permute-start | bytes 1179656 | tf_op jit(solution)/shard_map/ppermute | solution.py:139
  13.7 0.3 collective-permute-start.3
  14.1 2.6 %collective-permute-start = (s32[256,2]{0,1:T(2,128)S(1)}, s32[256,2]{0,1:T(2,128)S(1)}, u32[]{:S(2)}, u32[]{:S(2)}) collective-permute-start(s32[256,2]{0,1:T(2,128)S(1)} %copy-done.5), channel_id=1, source_target_pairs={{0,16},{2,18},{4,20},{6,22},{8,24},{10,26},{12,28},{14,30},{16,0},... | collective-permute-start | bytes 6152 | tf_op jit(solution)/shard_map/ppermute | solution.py:136
  16.7 0.3 collective-permute-start.1
  17.0 30.8 %collective-permute-done = s32[256,2]{0,1:T(2,128)S(1)} collective-permute-done((s32[256,2]{0,1:T(2,128)S(1)}, s32[256,2]{0,1:T(2,128)S(1)}, u32[]{:S(2)}, u32[]{:S(2)}) %collective-permute-start) | collective-permute-done | bytes 2080 | tf_op jit(solution)/shard_map/ppermute | solution.py:136
  47.9 2.0 %dispatch.2 = bf16[8,128,768]{2,1,0:T(8,128)(2,1)} custom-call(s32[1]{0:T(128)} %bitcast.1.base_ref, s32[2,256]{1,0:T(2,128)S(1)} %bitcast.82, f32[2,256]{1,0:T(2,128)S(1)} %bitcast.83, bf16[256,768]{1,0:T(8,128)(2,1)S(1)} %collective-permute-done.2.in_ref, bf16[256,768]{1,0:T(8,128)(2,1)S(1)} %collective-permute-done.3.grad_ref), custom_call_target="tpu_custom_call" | custom-call | flops 402653184 | bytes 2359296 | tf_op jit(solution)/shard_map/dispatch/pallas_call | solution.py:78
  49.8 6.3 %all-to-all-start = ((bf16[8,128,768]{2,1,0:T(8,128)(2,1)}), bf16[8,128,768]{2,1,0:T(8,128)(2,1)}, u32[]{:S(2)}, u32[]{:S(2)}) async-start(bf16[8,128,768]{2,1,0:T(8,128)(2,1)} %dispatch.2), calls=%async_computation | async-start | bytes 3145728 | tf_op jit(solution)/shard_map/all_to_all | solution.py:132
  56.2 3.4 %collective-permute-start.8 = (bf16[31,768]{1,0:T(8,128)(2,1)S(1)}, bf16[31,768]{1,0:T(8,128)(2,1)S(1)}, u32[]{:S(2)}, u32[]{:S(2)}) collective-permute-start(bf16[31,768]{1,0:T(8,128)(2,1)S(1)} %slice.242), channel_id=1, source_target_pairs={{2,0},{4,2},{6,4},{8,6},{10,8},{12,10},{14,12},{16,14},{18,16},{20... | collective-permute-start | bytes 142856 | tf_op jit(solution)/shard_map/ppermute | solution.py:199
  59.6 0.2 slice_reduce_fusion.31
  59.9 5.4 %copy.14 = bf16[192,8,2,768]{3,1,2,0:T(8,128)(2,1)} copy(bf16[192,8,2,768]{3,2,1,0:T(2,128)(2,1)} %bitcast.86) | data formatting | bytes 9437184
  65.3 9.5 %collective-permute-done.8 = bf16[31,768]{1,0:T(8,128)(2,1)S(1)} collective-permute-done((bf16[31,768]{1,0:T(8,128)(2,1)S(1)}, bf16[31,768]{1,0:T(8,128)(2,1)S(1)}, u32[]{:S(2)}, u32[]{:S(2)}) %collective-permute-start.8) | collective-permute-done | bytes 47648 | tf_op jit(solution)/shard_map/ppermute | solution.py:199
  75.0 4.7 %fusion.15 = f32[512,1536]{1,0:T(8,128)} fusion(bf16[512,768]{1,0:T(8,128)(2,1)S(1)} %bitcast.99, bf16[1,1536,1536]{2,1,0:T(8,128)(2,1)} %param.14, s32[]{:T(128)S(6)} %select_n.42), kind=kOutput, calls=%fused_computation.20 | convolution fusion | flops 1207959552 | bytes 6291460 | tf_op jit(solution)/shard_map/dot_general | solution.py:152
  79.7 4.8 %fusion.23 = f32[512,1536]{1,0:T(8,128)} fusion(bf16[512,768]{1,0:T(8,128)(2,1)S(1)} %bitcast.97, bf16[1,1536,1536]{2,1,0:T(8,128)(2,1)} %param.15, s32[]{:T(128)S(6)} %select_n.42), kind=kOutput, calls=%fused_computation.28 | convolution fusion | flops 1207959552 | bytes 6291460 | tf_op jit(solution)/shard_map/dot_general | solution.py:152
  84.6 0.5 collective-permute-start.4
  85.1 1.5 fusion.120
  86.6 3.2 %fusion.19 = f32[512,1536]{1,0:T(8,128)S(1)} fusion(bf16[512,768]{1,0:T(8,128)(2,1)S(1)} %bitcast.100, bf16[1,1536,1536]{2,1,0:T(8,128)(2,1)} %param.14, s32[]{:T(128)S(6)} %select_n.42), kind=kOutput, calls=%fused_computation.24 | convolution fusion | flops 1207959552 | bytes 6291460 | tf_op jit(solution)/shard_map/dot_general | solution.py:152
  89.8 3.1 %fusion.25 = f32[512,1536]{1,0:T(8,128)S(1)} fusion(bf16[512,768]{1,0:T(8,128)(2,1)S(1)} %bitcast.98, bf16[1,1536,1536]{2,1,0:T(8,128)(2,1)} %param.15, s32[]{:T(128)S(6)} %select_n.42), kind=kOutput, calls=%fused_computation.30 | convolution fusion | flops 1207959552 | bytes 6291460 | tf_op jit(solution)/shard_map/dot_general | solution.py:152
  93.0 1.6 %fusion.117 = (bf16[8,1,64,768]{3,2,1,0:T(8,128)(2,1)S(1)}, bf16[8,1,64,768]{3,2,1,0:T(8,128)(2,1)S(1)}) fusion(bf16[8,2,64,768]{3,2,1,0:T(8,128)(2,1)} %collective-permute-done.6), kind=kLoop, calls=%fused_computation.190 | loop fusion | bytes 3145728 | tf_op jit(solution)/shard_map/slice | solution.py:176
  94.7 0.7 copy-done.8
  95.3 1.4 convolution_add_fusion
  96.8 1.0 copy-done.13
  97.9 2.0 %fusion.5 = bf16[512,1536]{1,0:T(8,128)(2,1)S(1)} fusion(f32[512,1536]{1,0:T(8,128)S(1)} %convolution_add_fusion, f32[512,1536]{1,0:T(8,128)S(1)} %copy-done.13, bf16[512,768]{1,0:T(8,128)(2,1)S(1)} %bitcast.95, bf16[1,1536,1536]{2,1,0:T(8,128)(2,1)S(1)} %bitcast.104, s32[]{:T(128)S(6)} %select_n.43), kind=kOutput, calls=%fused_computation.9 | convolution fusion | flops 1215823872 | bytes 11010052 | tf_op jit(solution)/shard_map/dot_general | solution.py:152
  99.9 1.4 fusion.48
  101.5 1.4 convolution_add_fusion.2
  102.9 2.0 %fusion.4 = bf16[512,1536]{1,0:T(8,128)(2,1)S(1)} fusion(f32[512,1536]{1,0:T(8,128)S(1)} %convolution_add_fusion.2, f32[512,1536]{1,0:T(8,128)S(1)} %fusion.25, bf16[512,768]{1,0:T(8,128)(2,1)S(1)} %bitcast.96, bf16[1,1536,1536]{2,1,0:T(8,128)(2,1)S(1)} %bitcast.104, s32[]{:T(128)S(6)} %select_n.43), kind=kOutput, calls=%fused_computation.8 | convolution fusion | flops 1215823872 | bytes 11010052 | tf_op jit(solution)/shard_map/dot_general | solution.py:152
  104.9 1.4 fusion.45
  106.3 0.5 collective-permute-start.5
  106.8 1.8 %broadcast_select_fusion.1 = (bf16[256,768]{1,0:T(8,128)(2,1)S(1)}, bf16[256,768]{1,0:T(8,128)(2,1)}) fusion(bf16[256,768]{1,0:T(8,128)(2,1)S(1)} %copy-done.10, bf16[256,768]{1,0:T(8,128)(2,1)} %collective-permute-done.9, pred[]{:T(512)S(6)} %eq.40), kind=kLoop, calls=%fused_computation.136 | loop fusion | flops 393216 | bytes 1572865 | tf_op jit(solution)/shard_map/jit(_where)/select_n | solution.py:21
  108.6 1.6 %fusion.42.here_ref = bf16[512,768]{1,0:T(8,128)(2,1)S(1)} fusion(bf16[512,1536]{1,0:T(8,128)(2,1)S(1)} %fusion.5, bf16[1,1536,1536]{2,1,0:T(8,128)(2,1)S(1)} %bitcast.92, s32[]{:T(128)S(6)} %select_n.42), kind=kOutput, calls=%fused_computation.45 | convolution fusion | flops 1208352768 | bytes 4718596 | tf_op jit(solution)/shard_map/dot_general | solution.py:152
  110.2 1.4 fusion.39.here_ref
  111.7 1.0 finish.2.rest_0_
  112.7 1.0 finish.3
  113.7 5.6 %all-to-all-start.2 = ((bf16[16,64,768]{2,1,0:T(8,128)(2,1)}), bf16[16,64,768]{2,1,0:T(8,128)(2,1)S(1)}, u32[]{:S(2)}, u32[]{:S(2)}) async-start(bf16[16,64,768]{2,1,0:T(8,128)(2,1)} %bitcast.21), calls=%async_computation.2 | async-start | bytes 3145728 | tf_op jit(solution)/shard_map/all_to_all | solution.py:186
  119.4 3.9 %fusion.90 = f32[256,1536]{1,0:T(8,128)S(1)} fusion(bf16[1536,1536]{1,0:T(8,128)(2,1)} %bitcast.87, bf16[256,768]{1,0:T(8,128)(2,1)S(1)} %copy-done.11, bf16[256,768]{1,0:T(8,128)(2,1)S(1)} %get-tuple-element.46), kind=kOutput, calls=%fused_computation.124 | convolution fusion | flops 1209532416 | bytes 7077888 | tf_op jit(solution)/shard_map/dot_general | solution.py:197
  123.3 3.3 %multiply_convert_fusion = (bf16[256,768]{1,0:T(8,128)(2,1)S(1)}, f32[256,768]{1,0:T(8,128)S(1)}) fusion(f32[256,1536]{1,0:T(8,128)S(1)} %fusion.90, f32[287,768]{1,0:T(8,128)S(1)} %maximum_convert_fusion, f32[768]{0:T(1024)S(1)} %get-tuple-element.34, f32[768]{0:T(1024)S(1)} %get-tuple-element.35, f32[768]{0:T(1024)S(1)} %get-tuple-element.5, ...), kind=kLoop, calls=%fused_computation.132 | loop fusion | flops 13369344 | bytes 27230208 | tf_op jit(solution)/shard_map/convert
  126.6 0.2 fusion.55
  126.9 1.4 fusion.6
  128.4 0.2 fusion.52
  128.6 1.5 collective-permute-done.10
  130.3 0.9 copy.13
  131.2 25.4 %all-to-all-done.2 = bf16[16,64,768]{2,1,0:T(8,128)(2,1)S(1)} async-done(((bf16[16,64,768]{2,1,0:T(8,128)(2,1)}), bf16[16,64,768]{2,1,0:T(8,128)(2,1)S(1)}, u32[]{:S(2)}, u32[]{:S(2)}) %all-to-all-start.2) | async-done | bytes 1572896 | tf_op jit(solution)/shard_map/all_to_all | solution.py:186
  156.6 1.4 fusion.51
  (59 shorter events, 1.0 us)
Async XLA Ops:
  0.6 13.5 %copy-start.5 = (s32[256,2]{0,1:T(2,128)S(1)}, s32[256,2]{0,1:T(2,128)}, u32[]{:S(2)}) copy-start(s32[256,2]{0,1:T(2,128)} %param.12) | copy-start | bytes 6148
  0.6 16.0 %copy-start.7 = (f32[256,2]{0,1:T(2,128)S(1)}, f32[256,2]{0,1:T(2,128)}, u32[]{:S(2)}) copy-start(f32[256,2]{0,1:T(2,128)} %param.13) | copy-start | bytes 6148
  0.7 1.0 copy-start
  1.7 1.0 copy-start.2
  2.7 0.7 copy-start.4
  3.3 0.7 copy-start.6
  4.0 7.0 %copy-start.1 = (bf16[256,768]{1,0:T(8,128)(2,1)S(1)}, bf16[256,768]{1,0:T(8,128)(2,1)}, u32[]{:S(2)}) copy-start(bf16[256,768]{1,0:T(8,128)(2,1)} %in_ref.1) | copy-start | bytes 1179652
  4.0 9.7 %copy-start.3 = (bf16[256,768]{1,0:T(8,128)(2,1)S(1)}, bf16[256,768]{1,0:T(8,128)(2,1)}, u32[]{:S(2)}) copy-start(bf16[256,768]{1,0:T(8,128)(2,1)} %grad_ref.1) | copy-start | bytes 1179652
  5.9 43.9 %all-to-all-start.1 = ((bf16[8,128,768]{2,1,0:T(8,128)(2,1)}), bf16[8,128,768]{2,1,0:T(8,128)(2,1)S(1)}, u32[]{:S(2)}, u32[]{:S(2)}) async-start(bf16[8,128,768]{2,1,0:T(8,128)(2,1)} %dispatch.3), calls=%async_computation.1 | async-start | bytes 3145728 | tf_op jit(solution)/shard_map/all_to_all | solution.py:132
  11.1 45.1 %copy-start.10 = (bf16[256,768]{1,0:T(8,128)(2,1)S(1)}, bf16[256,768]{1,0:T(8,128)(2,1)}, u32[]{:S(2)}) copy-start(bf16[256,768]{1,0:T(8,128)(2,1)} %param.16) | copy-start | bytes 1179652
  11.1 45.1 %copy-start.9 = (bf16[256,768]{1,0:T(8,128)(2,1)S(1)}, bf16[256,768]{1,0:T(8,128)(2,1)}, u32[]{:S(2)}) copy-start(bf16[256,768]{1,0:T(8,128)(2,1)} %param.19) | copy-start | bytes 1179652
  11.1 48.5 %copy-start.12 = (f32[32,768]{1,0:T(8,128)S(1)}, f32[32,768]{1,0:T(8,128)}, u32[]{:S(2)}) copy-start(f32[32,768]{1,0:T(8,128)} %param.18) | copy-start | bytes 294916
  11.1 36.8 %collective-permute-start.2 = (bf16[256,768]{1,0:T(8,128)(2,1)S(1)}, bf16[256,768]{1,0:T(8,128)(2,1)S(1)}, u32[]{:S(2)}, u32[]{:S(2)}) collective-permute-start(bf16[256,768]{1,0:T(8,128)(2,1)S(1)} %copy-done.1), channel_id=1, source_target_pairs={{0,16},{2,18},{4,20},{6,22},{8,24},{10,26},{12,28},{14,30},{16,0},... | collective-permute-start | bytes 1179656 | tf_op jit(solution)/shard_map/ppermute | solution.py:139
  13.7 34.1 %collective-permute-start.3 = (bf16[256,768]{1,0:T(8,128)(2,1)S(1)}, bf16[256,768]{1,0:T(8,128)(2,1)S(1)}, u32[]{:S(2)}, u32[]{:S(2)}) collective-permute-start(bf16[256,768]{1,0:T(8,128)(2,1)S(1)} %copy-done.3), channel_id=1, source_target_pairs={{0,16},{2,18},{4,20},{6,22},{8,24},{10,26},{12,28},{14,30},{16,0},... | collective-permute-start | bytes 1179656 | tf_op jit(solution)/shard_map/ppermute | solution.py:140
  14.1 33.8 %collective-permute-start = (s32[256,2]{0,1:T(2,128)S(1)}, s32[256,2]{0,1:T(2,128)S(1)}, u32[]{:S(2)}, u32[]{:S(2)}) collective-permute-start(s32[256,2]{0,1:T(2,128)S(1)} %copy-done.5), channel_id=1, source_target_pairs={{0,16},{2,18},{4,20},{6,22},{8,24},{10,26},{12,28},{14,30},{16,0},... | collective-permute-start | bytes 6152 | tf_op jit(solution)/shard_map/ppermute | solution.py:136
  16.7 31.2 %collective-permute-start.1 = (f32[256,2]{0,1:T(2,128)S(1)}, f32[256,2]{0,1:T(2,128)S(1)}, u32[]{:S(2)}, u32[]{:S(2)}) collective-permute-start(f32[256,2]{0,1:T(2,128)S(1)} %copy-done.7), channel_id=1, source_target_pairs={{0,16},{2,18},{4,20},{6,22},{8,24},{10,26},{12,28},{14,30},{16,0},... | collective-permute-start | bytes 6152 | tf_op jit(solution)/shard_map/ppermute | solution.py:137
  49.8 34.7 %all-to-all-start = ((bf16[8,128,768]{2,1,0:T(8,128)(2,1)}), bf16[8,128,768]{2,1,0:T(8,128)(2,1)}, u32[]{:S(2)}, u32[]{:S(2)}) async-start(bf16[8,128,768]{2,1,0:T(8,128)(2,1)} %dispatch.2), calls=%async_computation | async-start | bytes 3145728 | tf_op jit(solution)/shard_map/all_to_all | solution.py:132
  56.1 50.7 %collective-permute-start.9 = (bf16[256,768]{1,0:T(8,128)(2,1)S(1)}, bf16[256,768]{1,0:T(8,128)(2,1)}, u32[]{:S(2)}, u32[]{:S(2)}) collective-permute-start(bf16[256,768]{1,0:T(8,128)(2,1)S(1)} %copy-done.10), channel_id=1, source_target_pairs={{0,1},{1,0},{2,3},{3,2},{4,5},{5,4},{6,7},{7,6},{8,9},{9,8},{10,11... | collective-permute-start | bytes 1179656 | tf_op jit(solution)/shard_map/ppermute | solution.py:13
  56.2 18.6 %collective-permute-start.8 = (bf16[31,768]{1,0:T(8,128)(2,1)S(1)}, bf16[31,768]{1,0:T(8,128)(2,1)S(1)}, u32[]{:S(2)}, u32[]{:S(2)}) collective-permute-start(bf16[31,768]{1,0:T(8,128)(2,1)S(1)} %slice.242), channel_id=1, source_target_pairs={{2,0},{4,2},{6,4},{8,6},{10,8},{12,10},{14,12},{16,14},{18,16},{20... | collective-permute-start | bytes 142856 | tf_op jit(solution)/shard_map/ppermute | solution.py:199
  74.8 18.2 %collective-permute-start.6 = (bf16[8,2,64,768]{3,2,1,0:T(8,128)(2,1)S(1)}, bf16[8,2,64,768]{3,2,1,0:T(8,128)(2,1)}, u32[]{:S(2)}, u32[]{:S(2)}) collective-permute-start(bf16[8,2,64,768]{3,2,1,0:T(8,128)(2,1)S(1)} %bitcast.84), channel_id=1, source_target_pairs={{0,1},{1,0},{2,3},{3,2},{4,5},{5,4},{6,7},{7,6},{8,9},{9,8},{10,11... | collective-permute-start | bytes 4718600 | tf_op jit(solution)/shard_map/ppermute | solution.py:13
  84.6 16.8 %collective-permute-start.4 = (bf16[8,2,64,768]{3,2,1,0:T(8,128)(2,1)}, bf16[8,2,64,768]{3,2,1,0:T(8,128)(2,1)S(1)}, u32[]{:S(2)}, u32[]{:S(2)}) collective-permute-start(bf16[8,2,64,768]{3,2,1,0:T(8,128)(2,1)} %bitcast.4), channel_id=1, source_target_pairs={{0,1},{1,0},{2,3},{3,2},{4,5},{5,4},{6,7},{7,6},{8,9},{9,8},{10,11... | collective-permute-start | bytes 4718600 | tf_op jit(solution)/shard_map/ppermute | solution.py:13
  86.6 8.1 %slice-start.2 = ((s8[4718592]{0:T(1024)(128)(4,1)}), s8[4194304]{0:T(1024)(128)(4,1)S(1)}, s32[]{:S(2)}) async-start(s8[4718592]{0:T(1024)(128)(4,1)} %bitcast.91), calls=%async_computation.5 | async-start | bytes 8388608
  89.8 4.8 %slice-start.3 = ((s8[4718592]{0:T(1024)(128)(4,1)}), s8[524288]{0:T(1024)(128)(4,1)S(1)}, s32[]{:S(2)}) async-start(s8[4718592]{0:T(1024)(128)(4,1)} %bitcast.91), calls=%async_computation.6 | async-start | bytes 1048576
  93.0 2.4 %copy-start.8 = (f32[512,1536]{1,0:T(8,128)S(1)}, f32[512,1536]{1,0:T(8,128)}, u32[]{:S(2)}) copy-start(f32[512,1536]{1,0:T(8,128)} %fusion.15) | copy-start | bytes 9437188
  93.0 3.8 %slice-start.4 = ((s8[4718592]{0:T(1024)(128)(4,1)}), s8[4194304]{0:T(1024)(128)(4,1)S(1)}, s32[]{:S(2)}) async-start(s8[4718592]{0:T(1024)(128)(4,1)} %bitcast.103), calls=%async_computation.7 | async-start | bytes 8388608
  95.3 1.5 slice-start.5
  95.3 2.5 %copy-start.13 = (f32[512,1536]{1,0:T(8,128)S(1)}, f32[512,1536]{1,0:T(8,128)}, u32[]{:S(2)}) copy-start(f32[512,1536]{1,0:T(8,128)} %fusion.23) | copy-start | bytes 9437188
  101.3 10.4 %collective-permute-start.7 = (bf16[512,768]{1,0:T(8,128)(2,1)S(1)}, bf16[512,768]{1,0:T(8,128)(2,1)S(1)}, u32[]{:S(2)}, u32[]{:S(2)}) collective-permute-start(bf16[512,768]{1,0:T(8,128)(2,1)S(1)} %fusion.48), channel_id=1, source_target_pairs={{0,1},{1,0},{2,3},{3,2},{4,5},{5,4},{6,7},{7,6},{8,9},{9,8},{10,11... | collective-permute-start | bytes 2359304 | tf_op jit(solution)/shard_map/ppermute | solution.py:13
  106.3 6.4 %collective-permute-start.5 = (bf16[512,768]{1,0:T(8,128)(2,1)S(1)}, bf16[512,768]{1,0:T(8,128)(2,1)S(1)}, u32[]{:S(2)}, u32[]{:S(2)}) collective-permute-start(bf16[512,768]{1,0:T(8,128)(2,1)S(1)} %fusion.45), channel_id=1, source_target_pairs={{0,1},{1,0},{2,3},{3,2},{4,5},{5,4},{6,7},{7,6},{8,9},{9,8},{10,11... | collective-permute-start | bytes 2359304 | tf_op jit(solution)/shard_map/ppermute | solution.py:13
  112.7 6.7 %copy-start.11 = (bf16[256,768]{1,0:T(8,128)(2,1)S(1)}, bf16[256,768]{1,0:T(8,128)(2,1)}, u32[]{:S(2)}) copy-start(bf16[256,768]{1,0:T(8,128)(2,1)} %get-tuple-element.47) | copy-start | bytes 1179652
  113.7 42.9 %all-to-all-start.2 = ((bf16[16,64,768]{2,1,0:T(8,128)(2,1)}), bf16[16,64,768]{2,1,0:T(8,128)(2,1)S(1)}, u32[]{:S(2)}, u32[]{:S(2)}) async-start(bf16[16,64,768]{2,1,0:T(8,128)(2,1)} %bitcast.21), calls=%async_computation.2 | async-start | bytes 3145728 | tf_op jit(solution)/shard_map/all_to_all | solution.py:186
  119.4 7.5 %slice-start = ((s8[4718592]{0:T(1024)(128)(4,1)}), s8[4194304]{0:T(1024)(128)(4,1)S(1)}, s32[]{:S(2)}) async-start(s8[4718592]{0:T(1024)(128)(4,1)} %bitcast.88), calls=%async_computation.3 | async-start | bytes 8388608
  123.3 3.6 %slice-start.1 = ((s8[4718592]{0:T(1024)(128)(4,1)}), s8[524288]{0:T(1024)(128)(4,1)S(1)}, s32[]{:S(2)}) async-start(s8[4718592]{0:T(1024)(128)(4,1)} %bitcast.88), calls=%async_computation.4 | async-start | bytes 1048576
  128.3 1.8 %collective-permute-start.10 = (bf16[768,256]{0,1:T(8,128)(2,1)S(1)}, bf16[768,256]{0,1:T(8,128)(2,1)S(1)}, u32[]{:S(2)}, u32[]{:S(2)}) collective-permute-start(bf16[768,256]{0,1:T(8,128)(2,1)S(1)} %broadcast_select_fusion.2), channel_id=1, source_target_pairs={{0,1},{1,0},{2,3},{3,2},{4,5},{5,4},{6,7},{7,6},{8,9},{9,8},{10,11... | collective-permute-start | bytes 1179656 | tf_op jit(solution)/shard_map/ppermute | solution.py:13

commit v2 on v1

v2 whole, which is shorter than its diff:
```python
import math
import jax
import jax.numpy as jnp
from jax import lax
from jax.experimental import pallas as pl
from jax.experimental.pallas import tpu as pltpu
from jax.sharding import PartitionSpec as P

BF = jnp.bfloat16
F32 = jnp.float32


def swap(x):
    return lax.ppermute(x, "tensor", [(0, 1), (1, 0)])


def gather_channels(x):
    if lax.axis_size("tensor") != 2:
        return lax.all_gather(x, "tensor", axis=1, tiled=True)
    other = swap(x)
    first = lax.axis_index("tensor") == 0
    return jnp.concatenate([jnp.where(first, x, other), jnp.where(first, other, x)], axis=1)


def scatter_sum(term, axis):
    if lax.axis_size("tensor") != 2:
        return lax.psum_scatter(term, "tensor", scatter_dimension=axis, tiled=True)
    first = lax.axis_index("tensor") == 0
    low, high = jnp.split(term, 2, axis=axis)
    other = swap(jnp.where(first, high, low))
    own = jnp.where(first, low, high)
    return (own.astype(F32) + other.astype(F32)).astype(BF)


def slots(r_ref_0, r_ref_1, experts):
    frames = experts.shape[1]
    one = r_ref_0 == experts
    named = jnp.where(one, 1.0, jnp.where(r_ref_1 == experts, 1.0, 0.0))
    before = lax.broadcasted_iota(jnp.int32, (frames, frames), 0) < lax.broadcasted_iota(
        jnp.int32, (frames, frames), 1
    )
    count = jnp.dot(named.astype(BF), jnp.where(before, 1.0, 0.0).astype(BF), preferred_element_type=F32)
    return jnp.where(named > 0.0, count.astype(jnp.int32), -1), one


def dispatch_kernel(origin_ref, r_ref, g_ref, in_ref, grad_ref, *outs):
    capacity, twice = outs[0].shape[-2:]
    channels = twice // 2
    number = len(outs) if len(outs) > 1 else outs[0].shape[0]
    frames = r_ref.shape[1]
    experts = origin_ref[0] ^ lax.broadcasted_iota(jnp.int32, (number, frames), 0)
    slot, one = slots(r_ref[0:1, :], r_ref[1:2, :], experts)
    gate = jnp.where(one, g_ref[0:1, :], g_ref[1:2, :])
    place = lax.broadcasted_iota(jnp.int32, (number, capacity, frames), 1)
    hot = jnp.broadcast_to(slot[:, None, :], place.shape) == place
    scale = jnp.sum(jnp.where(hot, jnp.broadcast_to(gate[:, None, :], place.shape), 0.0), axis=2, keepdims=True)
    hot = jnp.where(hot, 1.0, 0.0).reshape(number * capacity, frames).astype(BF)
    x = jnp.dot(hot, in_ref[...], preferred_element_type=F32).astype(BF).reshape(number, capacity, channels)
    g = jnp.dot(hot, grad_ref[...], preferred_element_type=F32).reshape(number, capacity, channels) * scale
    g = g.astype(BF)
    if len(outs) == 1:
        outs[0][:, :, :channels] = x
        outs[0][:, :, channels:] = g
    else:
        for i, out in enumerate(outs):
            out[:, :channels] = x[i]
            out[:, channels:] = g[i]


def dispatch(origin, number, capacity, r, g, in_rows, grad_rows, apart):
    frames, channels = in_rows.shape
    flops = 4 * number * capacity * frames * channels
    if apart:
        shape = (jax.ShapeDtypeStruct((capacity, 2 * channels), BF),) * number
        outs = [pl.BlockSpec((capacity, 2 * channels), lambda i: (0, 0))] * number
    else:
        shape = jax.ShapeDtypeStruct((number, capacity, 2 * channels), BF)
        outs = pl.BlockSpec(shape.shape, lambda i: (0, 0, 0))
    return pl.pallas_call(
        dispatch_kernel,
        grid=(1,),
        out_shape=shape,
        in_specs=[pl.BlockSpec(memory_space=pltpu.SMEM)]
        + [pl.BlockSpec(a.shape, lambda i: (0, 0)) for a in (r, g, in_rows, grad_rows)],
        out_specs=outs,
        cost_estimate=pl.CostEstimate(
            flops=flops, bytes_accessed=(64 if apart else 4) * channels * (frames + number * capacity), transcendentals=0
        ),
        compiler_params=pltpu.CompilerParams(vmem_limit_bytes=(16 if apart else 60) << 20),
        name="dispatch",
    )(origin.reshape(1), r, g, in_rows, grad_rows)


def gradient(first, second):
    sig = jax.nn.sigmoid(first)
    return (second * sig * (1.0 + first * (1.0 - sig))).astype(BF)


def times(a, w, over):
    return lax.dot_general(a, w, (((1,), (over,)), ((), ())), preferred_element_type=F32)


def warm_kernel(in_ref, out_ref, done_ref):
    done_ref[...] = jnp.zeros_like(done_ref)


def warm(w_in, w_out):
    return pl.pallas_call(
        warm_kernel,
        out_shape=jax.ShapeDtypeStruct((8, 128), F32),
        in_specs=[pl.BlockSpec(memory_space=pltpu.VMEM)] * 2,
        out_specs=pl.BlockSpec(memory_space=pltpu.VMEM),
        cost_estimate=pl.CostEstimate(flops=0, bytes_accessed=4096, transcendentals=0),
        compiler_params=pltpu.CompilerParams(vmem_limit_bytes=1 << 20),
        name="warm",
    )(w_in, w_out)


def expert_kernel(core_ref, own_ref, oth_ref, in_ref, out_ref, here_ref, away_ref, hidden):
    channels = own_ref.shape[1] // 2
    width = in_ref.shape[1]
    chunk = math.gcd(width, 512)
    piece = math.gcd(channels, 256)
    own = pl.multiple_of(core_ref[0] * channels, channels)
    oth = pl.multiple_of((1 - core_ref[0]) * channels, channels)
    for at in range(0, width, chunk):
        part = slice(at, at + chunk)
        one = times(own_ref[:, :channels], in_ref[pl.ds(own, channels), part], 0)
        one += times(oth_ref[:, :channels], in_ref[pl.ds(oth, channels), part], 0)
        two = times(own_ref[:, channels:], out_ref[part, pl.ds(own, channels)], 1)
        two += times(oth_ref[:, channels:], out_ref[part, pl.ds(oth, channels)], 1)
        hidden[:, part] = gradient(one, two)
    for ref, begin in ((away_ref, oth), (here_ref, own)):
        for at in range(0, channels, piece):
            rows = pl.ds(pl.multiple_of(begin + at, piece), piece)
            ref[:, at : at + piece] = times(hidden[...], in_ref[rows, :], 1).astype(BF)


def expert(core, own, oth, w_in, w_out):
    rows, channels = own.shape[0], own.shape[1] // 2
    width = w_in.shape[1]
    whole = pl.BlockSpec((rows, 2 * channels), lambda i: (0, 0))
    out = pl.BlockSpec((rows, channels), lambda i: (0, 0))
    shape = jax.ShapeDtypeStruct((rows, channels), BF)
    return pl.pallas_call(
        expert_kernel,
        grid=(1,),
        out_shape=(shape, shape),
        in_specs=[pl.BlockSpec(memory_space=pltpu.SMEM), whole, whole]
        + [pl.BlockSpec(memory_space=pltpu.VMEM)] * 2,
        out_specs=(out, out),
        scratch_shapes=[pltpu.VMEM((rows, width), BF)],
        cost_estimate=pl.CostEstimate(
            flops=12 * rows * channels * width,
            bytes_accessed=8 * width * channels + 12 * rows * channels,
            transcendentals=rows * width,
        ),
        compiler_params=pltpu.CompilerParams(vmem_limit_bytes=rows * (8 * width + 24 * channels) + (1 << 20)),
        name="expert",
    )(core.reshape(1), own, oth, w_in, w_out)


def finish_kernel(here_ref, back_ref, *outs):
    capacity = outs[0].shape[0]
    for i, out in enumerate(outs):
        part = slice(i * capacity, (i + 1) * capacity)
        out[...] = (here_ref[part].astype(F32) + back_ref[part].astype(F32)).astype(BF)


def finish(here, back, pieces):
    rows, channels = here.shape
    capacity = rows // pieces
    whole = pl.BlockSpec((rows, channels), lambda i: (0, 0))
    return pl.pallas_call(
        finish_kernel,
        grid=(1,),
        out_shape=(jax.ShapeDtypeStruct((capacity, channels), BF),) * pieces,
        in_specs=[whole] * 2,
        out_specs=[pl.BlockSpec((capacity, channels), lambda i: (0, 0))] * pieces,
        cost_estimate=pl.CostEstimate(
            flops=rows * channels, bytes_accessed=96 * rows * channels, transcendentals=0
        ),
        compiler_params=pltpu.CompilerParams(vmem_limit_bytes=16 * rows * channels),
        name="finish",
    )(here, back)


def join_kernel(*refs):
    capacity = refs[0].shape[0]
    for i in range(refs[-1].shape[0] // capacity):
        ref = refs[i]
        refs[-1][i * capacity : (i + 1) * capacity, :] = ref[...]


def join(parts, after=None):
    capacity, width = parts[0].shape
    rows = capacity * len(parts)
    extra = [] if after is None else [after]
    return pl.pallas_call(
        join_kernel,
        grid=(1,),
        out_shape=jax.ShapeDtypeStruct((rows, width), BF),
        in_specs=[pl.BlockSpec((capacity, width), lambda i: (0, 0))] * len(parts)
        + [pl.BlockSpec(a.shape, lambda i: (0, 0)) for a in extra],
        out_specs=pl.BlockSpec((rows, width), lambda i: (0, 0)),
        cost_estimate=pl.CostEstimate(flops=0, bytes_accessed=4 * rows * width, transcendentals=0),
        compiler_params=pltpu.CompilerParams(vmem_limit_bytes=8 << 20),
        name="join",
    )(*parts, *extra)


def combine_kernel(slot_ref, near_ref, *refs):
    out_ref, far = refs[-2:]
    capacity = refs[0].shape[0]
    number, frames = slot_ref.shape
    for i, ref in enumerate(refs[:-2]):
        far[i * capacity : (i + 1) * capacity, :] = ref[...]
    place = lax.broadcasted_iota(jnp.int32, (number, capacity, frames), 1)
    hot = jnp.broadcast_to(slot_ref[...][:, None, :], place.shape) == place
    hot = jnp.where(hot, 1.0, 0.0).reshape(number * capacity, frames).astype(BF)
    half = number * capacity // 2

    def gathered(rows, picks):
        return lax.dot_general(rows, picks, (((0,), (0,)), ((), ())), preferred_element_type=F32)

    out_ref[...] = (gathered(near_ref[...], hot[:half]) + gathered(far[...], hot[half:])).astype(BF)


def combine(slot, near, parts):
    _, frames = slot.shape
    rows, channels = near.shape
    return pl.pallas_call(
        combine_kernel,
        grid=(1,),
        out_shape=jax.ShapeDtypeStruct((channels, frames), BF),
        in_specs=[pl.BlockSpec(a.shape, lambda i: (0, 0)) for a in (slot, near, *parts)],
        out_specs=pl.BlockSpec((channels, frames), lambda i: (0, 0)),
        scratch_shapes=[pltpu.VMEM((rows, channels), BF)],
        cost_estimate=pl.CostEstimate(
            flops=4 * rows * channels * frames, bytes_accessed=6 * rows * channels, transcendentals=0
        ),
        compiler_params=pltpu.CompilerParams(vmem_limit_bytes=12 << 20),
        name="combine",
    )(slot, near, *parts)


def body(moe_in, moe_grad, routes, gates, w_in, w_out, conv_in, w_glu, kernel, conv_grad):
    frames, channels = moe_in.shape
    sources = lax.axis_size("expert")
    half = sources // 2
    quarter = half // 2
    capacity = 4 * frames // sources
    model = w_in.shape[1]
    w_in, w_out = w_in[0], w_out[0]
    me = lax.axis_index("expert")
    base = me & half
    halves = [list(range(half)), list(range(half, sources))]

    def flip(x, by):
        return lax.ppermute(x, "expert", [(i, i ^ by) for i in range(sources)])

    def in_half(rows):
        return lax.all_to_all(
            rows, "expert", split_axis=0, concat_axis=0, tiled=True, axis_index_groups=halves
        )

    far_routes = flip(routes, half).T
    far_gates = flip(gates, half).T
    routes_t, gates_t = routes.T, gates.T
    far_in = flip(moe_in, half)
    far_grad = flip(moe_grad, half)

    both = dispatch(base, half, capacity, routes_t, gates_t, moe_in, moe_grad, False)
    near_rows = in_half(both).reshape(half * capacity, 2 * channels)
    sent = dispatch(me, half, capacity, far_routes, far_gates, far_in, far_grad, True)
    arrived = [sent[0]]
    for k in range(1, half):
        arrived.append(flip(sent[k], k))

    def share(own, pieces):
        if lax.axis_size("tensor") != 2:
            x = gather_channels(own[:, :channels])
            g = gather_channels(own[:, channels:])
            pre_grad = gradient(times(x, w_in, 0), times(g, w_out, 1))
            part = scatter_sum(times(pre_grad, w_in, 1).astype(BF), 1)
            return jnp.split(part, pieces, axis=0)
        core = lax.axis_index("tensor")
        oth = swap(own)
        here, away = expert(core, own, oth, w_in, w_out)
        back = swap(away)
        return finish(here, back, pieces)

    ready = warm(w_in, w_out)
    plane = join(arrived[:quarter], ready)
    beyond = join(arrived[quarter:])
    far_grads = list(share(plane, quarter))
    (near_grads,) = share(near_rows, 1)
    far_grads += list(share(beyond, half - quarter))

    returned = [in_half(near_grads.reshape(half, capacity, channels)).reshape(half * capacity, channels)]
    for k in range(half):
        returned.append(flip(far_grads[k], half ^ k))
    order = lax.broadcasted_iota(jnp.int32, (sources, frames), 0)
    experts = jnp.where(order < half, base, me) ^ order
    slot, _ = slots(routes_t[0:1], routes_t[1:2], experts)
    moe_input_grad = combine(slot, returned[0], returned[1:])

    conv_wide = gather_channels(conv_in)
    glu_weight = w_glu.reshape(model, 2 * channels)
    glu_pre = jnp.dot(conv_wide, glu_weight, preferred_element_type=F32)
    taps = kernel.shape[0]
    future = lax.ppermute(conv_grad[: taps - 1], "expert", [(i, i - 1) for i in range(1, sources)])
    extended = jnp.concatenate([conv_grad, future], axis=0).astype(F32)
    mix_grad = jnp.zeros((frames, channels), F32)
    for offset in range(taps):
        mix_grad = mix_grad + kernel[offset] * extended[offset : offset + frames]
    value = glu_pre[:, :channels]
    gate = glu_pre[:, channels:]
    sig_gate = jax.nn.sigmoid(gate)
    glu_grad = jnp.concatenate([mix_grad * sig_gate, mix_grad * value * sig_gate * (1.0 - sig_gate)], axis=1).astype(BF)
    term = lax.dot_general(
        glu_weight, glu_grad, (((1,), (1,)), ((), ())), preferred_element_type=F32
    ).astype(BF)
    conv_input_grad = scatter_sum(term, 0)
    return (moe_input_grad, conv_input_grad)


def solution(mesh):
    placed = (
        P("expert", "tensor"),
        P("expert", "tensor"),
        P("expert", None),
        P("expert", None),
        P("expert", None, "tensor"),
        P("expert", "tensor", None),
        P("expert", "tensor"),
        P(None, None, "tensor"),
        P(None, "tensor"),
        P("expert", "tensor"),
    )

    return jax.shard_map(
        body,
        mesh=mesh,
        in_specs=placed,
        out_specs=(P("tensor", "expert"), P("tensor", "expert")),
        check_vma=False,
    )
```

time: 159 us -> 149 us (0.937)
  the two profiles are of different devices: /device:TPU:12 before, /device:TPU:0 now
where the time goes in v2:
time: 149 us; the launch traced here: 148 us
  starting transfers between devices  69.5 us (47%)
  Pallas kernels  24.3 us (16%)
  local copies, waits for them, and re-layouts  23.1 us (16%)
  waiting for transfers between devices  15.3 us (10%)
  other arithmetic  8.44 us (6%)
  matrix products  5.62 us (4%)
    ppermute x19, starting transfers between devices, flip(): return lax.ppermute(x, 'expert', [(i, i ^ by) for i in range(sources)])  56.2 us
    unnamed x102, local copies, waits for them, and re-layouts  17.9 us
    pallas_call x3, Pallas kernels, expert(): pl.pallas_call(expert_kernel, grid=(1,), out_shape=(shape, shape), in_spe...  17 us
    ppermute x19, waiting for transfers between devices, flip(): return lax.ppermute(x, 'expert', [(i, i ^ by) for i in range(sources)])  15.3 us
    all_to_all x2, starting transfers between devices, in_half(): lax.all_to_all(rows, 'expert', split_axis=0, concat_axis=0, tiled=True, a...  10.1 us
    pallas_call x2, Pallas kernels, dispatch(): pl.pallas_call(dispatch_kernel, grid=(1,), out_shape=shape, in_specs=[pl....  4.63 us
    dot_general x1, matrix products, body(): glu_pre = jnp.dot(conv_wide, glu_weight, preferred_element_type=F32)  4.03 us
    slice x2, local copies, waits for them, and re-layouts, body(): mix_grad = mix_grad + kernel[offset] * extended[offset:offset + frames]  3.86 us
  transfers between devices with their start and end apart: 30, of which 6 were waited for; matrix products, arithmetic and copies ran while one was open for 17% of the time, Pallas kernels for 13%

profile of v2, /device:TPU:0, one launch (start us, length us, event | category | flops | bytes accessed | tf_op | source)
XLA Modules:
  0.0 147.8 jit_solution(15939571950434771841)
XLA Ops:
  0.6 3.1 %dispatch.2 = bf16[8,64,1536]{2,1,0:T(8,128)(2,1)} custom-call(s32[1]{0:T(128)} %bitcast.4.origin_ref, s32[2,256]{1,0:T(2,128)} %bitcast.r_ref, f32[2,256]{1,0:T(2,128)} %bitcast.42, bf16[256,768]{1,0:T(8,128)(2,1)} %in_ref.1, bf16[256,768]{1,0:T(8,128)(2,1)} %grad_ref.1), custom_call_target="tpu_custom_call" | custom-call | flops 402653184 | bytes 2359296 | tf_op jit(solution)/shard_map/dispatch/pallas_call | solution.py:79
  3.7 6.3 %all-to-all-start = ((bf16[8,64,1536]{2,1,0:T(8,128)(2,1)}), bf16[8,64,1536]{2,1,0:T(8,128)(2,1)S(1)}, u32[]{:S(2)}, u32[]{:S(2)}) async-start(bf16[8,64,1536]{2,1,0:T(8,128)(2,1)} %dispatch.2), calls=%async_computation | async-start | bytes 3145728 | tf_op jit(solution)/shard_map/all_to_all | solution.py:263
  10.0 2.6 %collective-permute-start.4 = (bf16[256,768]{1,0:T(8,128)(2,1)}, bf16[256,768]{1,0:T(8,128)(2,1)S(1)}, u32[]{:S(2)}, u32[]{:S(2)}) collective-permute-start(bf16[256,768]{1,0:T(8,128)(2,1)} %in_ref.1), channel_id=1, source_target_pairs={{0,16},{2,18},{4,20},{6,22},{8,24},{10,26},{12,28},{14,30},{16,0},... | collective-permute-start | bytes 1179656 | tf_op jit(solution)/shard_map/ppermute | solution.py:260
  13.0 2.6 %collective-permute-start.2 = (s32[256,2]{0,1:T(2,128)}, s32[256,2]{0,1:T(2,128)S(1)}, u32[]{:S(2)}, u32[]{:S(2)}) collective-permute-start(s32[256,2]{0,1:T(2,128)} %param.12), channel_id=1, source_target_pairs={{0,16},{2,18},{4,20},{6,22},{8,24},{10,26},{12,28},{14,30},{16,0},... | collective-permute-start | bytes 6152 | tf_op jit(solution)/shard_map/ppermute | solution.py:260
  16.2 1.3 collective-permute-start.25
  17.5 2.1 %slice_reduce_fusion.31 = (f32[768]{0:T(1024)S(1)}, f32[768]{0:T(1024)S(1)}, f32[768]{0:T(1024)}, f32[768]{0:T(1024)}, f32[768]{0:T(1024)}, /*index=5*/f32[768]{...) fusion(f32[32,768]{1,0:T(8,128)} %param.18), kind=kLoop, calls=%fused_computation.131 | loop fusion | bytes 116736 | tf_op jit(solution)/shard_map/slice | solution.py:316
  19.6 1.7 %slice_reduce_fusion.30 = (f32[768]{0:T(1024)}, f32[768]{0:T(1024)}, f32[768]{0:T(1024)}, f32[768]{0:T(1024)}, f32[768]{0:T(1024)}, /*index=5*/f32[768]{0:T(1024...) fusion(f32[32,768]{1,0:T(8,128)} %param.18), kind=kLoop, calls=%fused_computation.130 | loop fusion | bytes 79872 | tf_op jit(solution)/shard_map/slice | solution.py:316
  21.3 5.4 %copy.13 = bf16[192,8,2,768]{3,1,2,0:T(8,128)(2,1)} copy(bf16[192,8,2,768]{3,2,1,0:T(2,128)(2,1)} %bitcast.37) | data formatting | bytes 9437184
  26.7 2.3 %copy-done = bf16[1,1536,1536]{2,1,0:T(8,128)(2,1)S(1)} copy-done((bf16[1,1536,1536]{2,1,0:T(8,128)(2,1)S(1)}, bf16[1,1536,1536]{2,1,0:T(8,128)(2,1)}, u32[]{:S(2)}) %copy-start) | copy-done | bytes 4718616
  29.1 2.3 %copy-done.2 = bf16[1,1536,1536]{2,1,0:T(8,128)(2,1)S(1)} copy-done((bf16[1,1536,1536]{2,1,0:T(8,128)(2,1)S(1)}, bf16[1,1536,1536]{2,1,0:T(8,128)(2,1)}, u32[]{:S(2)}) %copy-start.2) | copy-done | bytes 4718616
  31.4 0.7 copy-done.43
  32.1 5.9 %collective-permute-start.3 = (f32[256,2]{0,1:T(2,128)S(1)}, f32[256,2]{0,1:T(2,128)S(1)}, u32[]{:S(2)}, u32[]{:S(2)}) collective-permute-start(f32[256,2]{0,1:T(2,128)S(1)} %copy-done.43), channel_id=1, source_target_pairs={{0,16},{2,18},{4,20},{6,22},{8,24},{10,26},{12,28},{14,30},{16,0},... | collective-permute-start | bytes 6152 | tf_op jit(solution)/shard_map/ppermute | solution.py:260
  38.0 1.8 %maximum_convert_fusion = f32[287,768]{1,0:T(8,128)} fusion(bf16[31,768]{1,0:T(8,128)(2,1)} %collective-permute-done.25, bf16[256,768]{1,0:T(8,128)(2,1)S(1)} %copy-done.11), kind=kLoop, calls=%fused_computation.84 | loop fusion | flops 881664 | bytes 1322496 | tf_op jit(solution)/shard_map/convert_element_type | solution.py:313
  39.8 4.5 %collective-permute-done.2 = s32[256,2]{0,1:T(2,128)S(1)} collective-permute-done((s32[256,2]{0,1:T(2,128)}, s32[256,2]{0,1:T(2,128)S(1)}, u32[]{:S(2)}, u32[]{:S(2)}) %collective-permute-start.2) | collective-permute-done | bytes 2080 | tf_op jit(solution)/shard_map/ppermute | solution.py:260
  44.2 1.6 %dispatch.3 = (bf16[64,1536]{1,0:T(8,128)(2,1)S(1)}, bf16[64,1536]{1,0:T(8,128)(2,1)S(1)}, bf16[64,1536]{1,0:T(8,128)(2,1)S(1)}, bf16[64,1536]{1,0:T(8,128)(2,1)...) custom-call(s32[1]{0:T(128)} %bitcast.11.origin_ref, ...), custom_call_target="tpu_custom_call" | custom-call | flops 402653184 | bytes 37748736 | tf_op jit(solution)/shard_map/dispatch/pallas_call | solution.py:79
  45.8 0.7 copy-done.4
  46.5 0.7 copy-done.6
  47.2 7.1 %collective-permute-start.15 = (bf16[64,1536]{1,0:T(8,128)(2,1)}, bf16[64,1536]{1,0:T(8,128)(2,1)S(1)}, u32[]{:S(2)}, u32[]{:S(2)}) collective-permute-start(bf16[64,1536]{1,0:T(8,128)(2,1)} %get-tuple-element.36), channel_id=1, source_target_pairs={{0,8},{2,10},{4,12},{6,14},{8,0},{10,2},{12,4},{14,6},{16,24},{18,... | collective-permute-start | bytes 589832 | tf_op jit(solution)/shard_map/ppermute | solution.py:260
  54.3 4.3 %collective-permute-start.17 = (bf16[64,1536]{1,0:T(8,128)(2,1)}, bf16[64,1536]{1,0:T(8,128)(2,1)S(1)}, u32[]{:S(2)}, u32[]{:S(2)}) collective-permute-start(bf16[64,1536]{1,0:T(8,128)(2,1)} %get-tuple-element.38), channel_id=1, source_target_pairs={{0,12},{2,14},{4,8},{6,10},{8,4},{10,6},{12,0},{14,2},{16,28},{18,... | collective-permute-start | bytes 589832 | tf_op jit(solution)/shard_map/ppermute | solution.py:260
  58.6 0.9 broadcast_select_fusion.1
  59.9 4.0 %fusion.39 = f32[256,1536]{1,0:T(8,128)S(1)} fusion(bf16[1536,1536]{1,0:T(8,128)(2,1)} %bitcast.38, bf16[256,768]{1,0:T(8,128)(2,1)} %get-tuple-element.83, bf16[256,768]{1,0:T(8,128)(2,1)} %get-tuple-element.82), kind=kOutput, calls=%fused_computation.75 | convolution fusion | flops 1209532416 | bytes 7077888 | tf_op jit(solution)/shard_map/dot_general | solution.py:310
  64.3 3.5 %multiply_convert_fusion = (bf16[256,768]{1,0:T(8,128)(2,1)S(1)}, f32[256,768]{1,0:T(8,128)S(1)}) fusion(f32[256,1536]{1,0:T(8,128)S(1)} %fusion.39, f32[287,768]{1,0:T(8,128)S(1)} %copy-done.8, f32[768]{0:T(1024)S(1)} %copy-done.41, f32[768]{0:T(1024)S(1)} %copy-done.42, f32[768]{0:T(1024)S(1)} %get-tuple-element.49, f32[768]{0:T(1024)S(1)} %copy-done.13, ...), kind=kLoop, calls=%fused_computation.83 | loop fusion | flops 13369344 | bytes 27230208 | tf_op jit(solution)/shard_map/convert
  67.8 1.5 %collective-permute-start.6 = (bf16[64,1536]{1,0:T(8,128)(2,1)S(1)}, bf16[64,1536]{1,0:T(8,128)(2,1)S(1)}, u32[]{:S(2)}, u32[]{:S(2)}) collective-permute-start(bf16[64,1536]{1,0:T(8,128)(2,1)S(1)} %copy-done.7), channel_id=1, source_target_pairs={{0,2},{2,0},{4,6},{6,4},{8,10},{10,8},{12,14},{14,12},{16,18},{18,... | collective-permute-start | bytes 589832 | tf_op jit(solution)/shard_map/ppermute | solution.py:260
  69.4 3.5 %collective-permute-start.7 = (bf16[64,1536]{1,0:T(8,128)(2,1)S(1)}, bf16[64,1536]{1,0:T(8,128)(2,1)S(1)}, u32[]{:S(2)}, u32[]{:S(2)}) collective-permute-start(bf16[64,1536]{1,0:T(8,128)(2,1)S(1)} %copy-done.5), channel_id=1, source_target_pairs={{0,4},{2,6},{4,0},{6,2},{8,12},{10,14},{12,8},{14,10},{16,20},{18,... | collective-permute-start | bytes 589832 | tf_op jit(solution)/shard_map/ppermute | solution.py:260
  72.8 2.2 %collective-permute-done.18.refs_3_ = bf16[64,1536]{1,0:T(8,128)(2,1)S(1)} collective-permute-done((bf16[64,1536]{1,0:T(8,128)(2,1)}, bf16[64,1536]{1,0:T(8,128)(2,1)S(1)}, u32[]{:S(2)}, u32[]{:S(2)}) %collective-permute-start.18) | collective-permute-done | bytes 196640 | tf_op jit(solution)/shard_map/ppermute | solution.py:260
  75.3 7.7 %expert.3 = (bf16[512,768]{1,0:T(8,128)(2,1)S(1)}, bf16[512,768]{1,0:T(8,128)(2,1)S(1)}) custom-call(s32[1]{0:T(128)} %bitcast.3.core_ref, bf16[512,1536]{1,0:T(8,128)(2,1)S(1)} %bitcast.34, bf16[512,1536]{1,0:T(8,128)(2,1)S(1)} %collective-permute-done.oth_ref, bf16[1536,1536]{1,0:T(8,128)(2,1)S(1)} %bitcast.23, bf16[1536,1536]{1,0:T(8,128)(2,1)S(1)} %bitcast.29), custom_call_target="tpu_custom_call" | custom-call | flops 7247757312 | bytes 14155776 | tf_op jit(solution)/shard_map/expert/pallas_call | solution.py:145
  84.0 1.4 fusion
  85.4 0.8 broadcast_select_fusion.2
  86.8 1.1 finish.3
  87.8 3.8 %all-to-all-start.1 = ((bf16[8,64,768]{2,1,0:T(8,128)(2,1)}), bf16[8,64,768]{2,1,0:T(8,128)(2,1)S(1)}, u32[]{:S(2)}, u32[]{:S(2)}) async-start(bf16[8,64,768]{2,1,0:T(8,128)(2,1)} %bitcast.9), calls=%async_computation.1 | async-start | bytes 1572864 | tf_op jit(solution)/shard_map/all_to_all | solution.py:263
  91.6 2.3 %copy-done.1 = bf16[1,1536,1536]{2,1,0:T(8,128)(2,1)S(1)} copy-done((bf16[1,1536,1536]{2,1,0:T(8,128)(2,1)S(1)}, bf16[1,1536,1536]{2,1,0:T(8,128)(2,1)}, u32[]{:S(2)}) %copy-start.1) | copy-done | bytes 4718616
  94.0 2.3 %copy-done.3 = bf16[1,1536,1536]{2,1,0:T(8,128)(2,1)S(1)} copy-done((bf16[1,1536,1536]{2,1,0:T(8,128)(2,1)S(1)}, bf16[1,1536,1536]{2,1,0:T(8,128)(2,1)}, u32[]{:S(2)}) %copy-start.3) | copy-done | bytes 4718616
  96.3 4.1 %expert.5 = (bf16[256,768]{1,0:T(8,128)(2,1)S(1)}, bf16[256,768]{1,0:T(8,128)(2,1)S(1)}) custom-call(s32[1]{0:T(128)} %bitcast.3.core_ref, bf16[256,1536]{1,0:T(8,128)(2,1)S(1)} %join.3.own_ref, bf16[256,1536]{1,0:T(8,128)(2,1)S(1)} %collective-permute-done.19.oth_ref, bf16[1536,1536]{1,0:T(8,128)(2,1)S(1)} %bitcast.24, bf16[1536,1536]{1,0:T(8,128)(2,1)S(1)} %bitcast.30), custom_call_target="tpu_custom_call" | custom-call | flops 3623878656 | bytes 11796480 | tf_op jit(solution)/shard_map/expert/pallas_call | solution.py:145
  100.5 5.2 %expert.4 = (bf16[256,768]{1,0:T(8,128)(2,1)S(1)}, bf16[256,768]{1,0:T(8,128)(2,1)S(1)}) custom-call(s32[1]{0:T(128)} %bitcast.3.core_ref, bf16[256,1536]{1,0:T(8,128)(2,1)S(1)} %join.2.own_ref, bf16[256,1536]{1,0:T(8,128)(2,1)} %collective-permute-done.9.oth_ref, bf16[1536,1536]{1,0:T(8,128)(2,1)S(1)} %bitcast.25, bf16[1536,1536]{1,0:T(8,128)(2,1)S(1)} %bitcast.31), custom_call_target="tpu_custom_call" | custom-call | flops 3623878656 | bytes 11796480 | tf_op jit(solution)/shard_map/expert/pallas_call | solution.py:145
  106.2 0.8 fusion.62
  107.1 3.4 %collective-permute-start.21 = (bf16[64,768]{1,0:T(8,128)(2,1)S(1)}, bf16[64,768]{1,0:T(8,128)(2,1)S(1)}, u32[]{:S(2)}, u32[]{:S(2)}) collective-permute-start(bf16[64,768]{1,0:T(8,128)(2,1)S(1)} %get-tuple-element.42), channel_id=1, source_target_pairs={{0,24},{2,26},{4,28},{6,30},{8,16},{10,18},{12,20},{14,22},{16,8},... | collective-permute-start | bytes 294920 | tf_op jit(solution)/shard_map/ppermute | solution.py:260
  110.5 1.6 %collective-permute-start.22 = (bf16[64,768]{1,0:T(8,128)(2,1)S(1)}, bf16[64,768]{1,0:T(8,128)(2,1)S(1)}, u32[]{:S(2)}, u32[]{:S(2)}) collective-permute-start(bf16[64,768]{1,0:T(8,128)(2,1)S(1)} %get-tuple-element.43), channel_id=1, source_target_pairs={{0,26},{2,24},{4,30},{6,28},{8,18},{10,16},{12,22},{14,20},{16,10}... | collective-permute-start | bytes 294920 | tf_op jit(solution)/shard_map/ppermute | solution.py:260
  112.1 4.0 %collective-permute-start.23 = (bf16[64,768]{1,0:T(8,128)(2,1)S(1)}, bf16[64,768]{1,0:T(8,128)(2,1)S(1)}, u32[]{:S(2)}, u32[]{:S(2)}) collective-permute-start(bf16[64,768]{1,0:T(8,128)(2,1)S(1)} %get-tuple-element.44), channel_id=1, source_target_pairs={{0,28},{2,30},{4,24},{6,26},{8,20},{10,22},{12,16},{14,18},{16,12}... | collective-permute-start | bytes 294920 | tf_op jit(solution)/shard_map/ppermute | solution.py:260
  117.0 11.8 %collective-permute-start.12 = (bf16[64,768]{1,0:T(8,128)(2,1)S(1)}, bf16[64,768]{1,0:T(8,128)(2,1)S(1)}, u32[]{:S(2)}, u32[]{:S(2)}) collective-permute-start(bf16[64,768]{1,0:T(8,128)(2,1)S(1)} %get-tuple-element.33), channel_id=1, source_target_pairs={{0,18},{2,16},{4,22},{6,20},{8,26},{10,24},{12,30},{14,28},{16,2},... | collective-permute-start | bytes 294920 | tf_op jit(solution)/shard_map/ppermute | solution.py:260
  128.8 2.0 %collective-permute-start.13 = (bf16[64,768]{1,0:T(8,128)(2,1)S(1)}, bf16[64,768]{1,0:T(8,128)(2,1)S(1)}, u32[]{:S(2)}, u32[]{:S(2)}) collective-permute-start(bf16[64,768]{1,0:T(8,128)(2,1)S(1)} %get-tuple-element.34), channel_id=1, source_target_pairs={{0,20},{2,22},{4,16},{6,18},{8,28},{10,30},{12,24},{14,26},{16,4},... | collective-permute-start | bytes 294920 | tf_op jit(solution)/shard_map/ppermute | solution.py:260
  130.7 5.1 %collective-permute-start.14 = (bf16[64,768]{1,0:T(8,128)(2,1)S(1)}, bf16[64,768]{1,0:T(8,128)(2,1)S(1)}, u32[]{:S(2)}, u32[]{:S(2)}) collective-permute-start(bf16[64,768]{1,0:T(8,128)(2,1)S(1)} %get-tuple-element.35), channel_id=1, source_target_pairs={{0,22},{2,20},{4,18},{6,16},{8,30},{10,28},{12,26},{14,24},{16,6},... | collective-permute-start | bytes 294920 | tf_op jit(solution)/shard_map/ppermute | solution.py:260
  135.8 1.1 add_convert_fusion
  136.9 0.9 copy.12
  137.8 1.2 collective-permute-done.11.refs_0_
  139.1 3.2 %collective-permute-done.12.refs_1_ = bf16[64,768]{1,0:T(8,128)(2,1)S(1)} collective-permute-done((bf16[64,768]{1,0:T(8,128)(2,1)S(1)}, bf16[64,768]{1,0:T(8,128)(2,1)S(1)}, u32[]{:S(2)}, u32[]{:S(2)}) %collective-permute-start.12) | collective-permute-done | bytes 98336 | tf_op jit(solution)/shard_map/ppermute | solution.py:260
  142.2 2.1 %collective-permute-done.13.refs_2_ = bf16[64,768]{1,0:T(8,128)(2,1)S(1)} collective-permute-done((bf16[64,768]{1,0:T(8,128)(2,1)S(1)}, bf16[64,768]{1,0:T(8,128)(2,1)S(1)}, u32[]{:S(2)}, u32[]{:S(2)}) %collective-permute-start.13) | collective-permute-done | bytes 98336 | tf_op jit(solution)/shard_map/ppermute | solution.py:260
  144.4 2.1 %collective-permute-done.14.refs_3_ = bf16[64,768]{1,0:T(8,128)(2,1)S(1)} collective-permute-done((bf16[64,768]{1,0:T(8,128)(2,1)S(1)}, bf16[64,768]{1,0:T(8,128)(2,1)S(1)}, u32[]{:S(2)}, u32[]{:S(2)}) %collective-permute-start.14) | collective-permute-done | bytes 98336 | tf_op jit(solution)/shard_map/ppermute | solution.py:260
  146.4 1.4 combine.1
  (143 shorter events, 4.4 us)
Async XLA Ops:
  3.7 11.9 %copy-start.12 = (bf16[256,768]{1,0:T(8,128)(2,1)S(1)}, bf16[256,768]{1,0:T(8,128)(2,1)}, u32[]{:S(2)}) copy-start(bf16[256,768]{1,0:T(8,128)(2,1)} %param.16) | copy-start | bytes 1179652
  3.7 11.9 %copy-start.11 = (bf16[256,768]{1,0:T(8,128)(2,1)S(1)}, bf16[256,768]{1,0:T(8,128)(2,1)}, u32[]{:S(2)}) copy-start(bf16[256,768]{1,0:T(8,128)(2,1)} %param.19) | copy-start | bytes 1179652
  3.7 55.9 %all-to-all-start = ((bf16[8,64,1536]{2,1,0:T(8,128)(2,1)}), bf16[8,64,1536]{2,1,0:T(8,128)(2,1)S(1)}, u32[]{:S(2)}, u32[]{:S(2)}) async-start(bf16[8,64,1536]{2,1,0:T(8,128)(2,1)} %dispatch.2), calls=%async_computation | async-start | bytes 3145728 | tf_op jit(solution)/shard_map/all_to_all | solution.py:263
  10.0 34.2 %collective-permute-start.4 = (bf16[256,768]{1,0:T(8,128)(2,1)}, bf16[256,768]{1,0:T(8,128)(2,1)S(1)}, u32[]{:S(2)}, u32[]{:S(2)}) collective-permute-start(bf16[256,768]{1,0:T(8,128)(2,1)} %in_ref.1), channel_id=1, source_target_pairs={{0,16},{2,18},{4,20},{6,22},{8,24},{10,26},{12,28},{14,30},{16,0},... | collective-permute-start | bytes 1179656 | tf_op jit(solution)/shard_map/ppermute | solution.py:260
  12.6 31.6 %collective-permute-start.5 = (bf16[256,768]{1,0:T(8,128)(2,1)}, bf16[256,768]{1,0:T(8,128)(2,1)S(1)}, u32[]{:S(2)}, u32[]{:S(2)}) collective-permute-start(bf16[256,768]{1,0:T(8,128)(2,1)} %grad_ref.1), channel_id=1, source_target_pairs={{0,16},{2,18},{4,20},{6,22},{8,24},{10,26},{12,28},{14,30},{16,0},... | collective-permute-start | bytes 1179656 | tf_op jit(solution)/shard_map/ppermute | solution.py:260
  13.0 31.3 %collective-permute-start.2 = (s32[256,2]{0,1:T(2,128)}, s32[256,2]{0,1:T(2,128)S(1)}, u32[]{:S(2)}, u32[]{:S(2)}) collective-permute-start(s32[256,2]{0,1:T(2,128)} %param.12), channel_id=1, source_target_pairs={{0,16},{2,18},{4,20},{6,22},{8,24},{10,26},{12,28},{14,30},{16,0},... | collective-permute-start | bytes 6152 | tf_op jit(solution)/shard_map/ppermute | solution.py:260
  15.6 43.1 %collective-permute-start.26 = (bf16[256,768]{1,0:T(8,128)(2,1)S(1)}, bf16[256,768]{1,0:T(8,128)(2,1)S(1)}, u32[]{:S(2)}, u32[]{:S(2)}) collective-permute-start(bf16[256,768]{1,0:T(8,128)(2,1)S(1)} %copy-done.12), channel_id=1, source_target_pairs={{0,1},{1,0},{2,3},{3,2},{4,5},{5,4},{6,7},{7,6},{8,9},{9,8},{10,11... | collective-permute-start | bytes 1179656 | tf_op jit(solution)/shard_map/ppermute | solution.py:14
  16.2 15.2 %collective-permute-start.25 = (bf16[31,768]{1,0:T(8,128)(2,1)}, bf16[31,768]{1,0:T(8,128)(2,1)}, u32[]{:S(2)}, u32[]{:S(2)}) collective-permute-start(bf16[31,768]{1,0:T(8,128)(2,1)} %slice.210), channel_id=1, source_target_pairs={{2,0},{4,2},{6,4},{8,6},{10,8},{12,10},{14,12},{16,14},{18,16},{20... | collective-permute-start | bytes 142856 | tf_op jit(solution)/shard_map/ppermute | solution.py:312
  32.1 12.1 %collective-permute-start.3 = (f32[256,2]{0,1:T(2,128)S(1)}, f32[256,2]{0,1:T(2,128)S(1)}, u32[]{:S(2)}, u32[]{:S(2)}) collective-permute-start(f32[256,2]{0,1:T(2,128)S(1)} %copy-done.43), channel_id=1, source_target_pairs={{0,16},{2,18},{4,20},{6,22},{8,24},{10,26},{12,28},{14,30},{16,0},... | collective-permute-start | bytes 6152 | tf_op jit(solution)/shard_map/ppermute | solution.py:260
  47.2 20.6 %collective-permute-start.15 = (bf16[64,1536]{1,0:T(8,128)(2,1)}, bf16[64,1536]{1,0:T(8,128)(2,1)S(1)}, u32[]{:S(2)}, u32[]{:S(2)}) collective-permute-start(bf16[64,1536]{1,0:T(8,128)(2,1)} %get-tuple-element.36), channel_id=1, source_target_pairs={{0,8},{2,10},{4,12},{6,14},{8,0},{10,2},{12,4},{14,6},{16,24},{18,... | collective-permute-start | bytes 589832 | tf_op jit(solution)/shard_map/ppermute | solution.py:260
  54.3 15.0 %collective-permute-start.16 = (bf16[64,1536]{1,0:T(8,128)(2,1)}, bf16[64,1536]{1,0:T(8,128)(2,1)S(1)}, u32[]{:S(2)}, u32[]{:S(2)}) collective-permute-start(bf16[64,1536]{1,0:T(8,128)(2,1)} %get-tuple-element.37), channel_id=1, source_target_pairs={{0,10},{2,8},{4,14},{6,12},{8,2},{10,0},{12,6},{14,4},{16,26},{18,... | collective-permute-start | bytes 589832 | tf_op jit(solution)/shard_map/ppermute | solution.py:260
  54.3 18.5 %collective-permute-start.17 = (bf16[64,1536]{1,0:T(8,128)(2,1)}, bf16[64,1536]{1,0:T(8,128)(2,1)S(1)}, u32[]{:S(2)}, u32[]{:S(2)}) collective-permute-start(bf16[64,1536]{1,0:T(8,128)(2,1)} %get-tuple-element.38), channel_id=1, source_target_pairs={{0,12},{2,14},{4,8},{6,10},{8,4},{10,6},{12,0},{14,2},{16,28},{18,... | collective-permute-start | bytes 589832 | tf_op jit(solution)/shard_map/ppermute | solution.py:260
  58.6 16.5 %collective-permute-start.18 = (bf16[64,1536]{1,0:T(8,128)(2,1)}, bf16[64,1536]{1,0:T(8,128)(2,1)S(1)}, u32[]{:S(2)}, u32[]{:S(2)}) collective-permute-start(bf16[64,1536]{1,0:T(8,128)(2,1)} %get-tuple-element.39), channel_id=1, source_target_pairs={{0,14},{2,12},{4,10},{6,8},{8,6},{10,4},{12,2},{14,0},{16,30},{18,... | collective-permute-start | bytes 589832 | tf_op jit(solution)/shard_map/ppermute | solution.py:260
  59.6 15.7 %collective-permute-start = (bf16[512,1536]{1,0:T(8,128)(2,1)S(1)}, bf16[512,1536]{1,0:T(8,128)(2,1)S(1)}, u32[]{:S(2)}, u32[]{:S(2)}) collective-permute-start(bf16[512,1536]{1,0:T(8,128)(2,1)S(1)} %bitcast.33), channel_id=1, source_target_pairs={{0,1},{1,0},{2,3},{3,2},{4,5},{5,4},{6,7},{7,6},{8,9},{9,8},{10,11... | collective-permute-start | bytes 4718600 | tf_op jit(solution)/shard_map/ppermute | solution.py:14
  59.6 4.4 %copy-start.13 = (f32[768]{0:T(1024)S(1)}, f32[768]{0:T(1024)}, u32[]{:S(2)}) copy-start(f32[768]{0:T(1024)} %get-tuple-element.50) | copy-start | bytes 9220
  59.6 4.4 %copy-start.14 = (f32[768]{0:T(1024)S(1)}, f32[768]{0:T(1024)}, u32[]{:S(2)}) copy-start(f32[768]{0:T(1024)} %get-tuple-element.51) | copy-start | bytes 9220
  59.6 4.4 %copy-start.15 = (f32[768]{0:T(1024)S(1)}, f32[768]{0:T(1024)}, u32[]{:S(2)}) copy-start(f32[768]{0:T(1024)} %get-tuple-element.52) | copy-start | bytes 9220
  59.6 4.4 %copy-start.16 = (f32[768]{0:T(1024)S(1)}, f32[768]{0:T(1024)}, u32[]{:S(2)}) copy-start(f32[768]{0:T(1024)} %get-tuple-element.53) | copy-start | bytes 9220
  59.6 4.4 %copy-start.17 = (f32[768]{0:T(1024)S(1)}, f32[768]{0:T(1024)}, u32[]{:S(2)}) copy-start(f32[768]{0:T(1024)} %get-tuple-element.54) | copy-start | bytes 9220
  59.6 4.4 %copy-start.18 = (f32[768]{0:T(1024)S(1)}, f32[768]{0:T(1024)}, u32[]{:S(2)}) copy-start(f32[768]{0:T(1024)} %get-tuple-element.55) | copy-start | bytes 9220
  59.6 4.4 %copy-start.19 = (f32[768]{0:T(1024)S(1)}, f32[768]{0:T(1024)}, u32[]{:S(2)}) copy-start(f32[768]{0:T(1024)} %get-tuple-element.56) | copy-start | bytes 9220
  59.6 4.4 %copy-start.20 = (f32[768]{0:T(1024)S(1)}, f32[768]{0:T(1024)}, u32[]{:S(2)}) copy-start(f32[768]{0:T(1024)} %get-tuple-element.57) | copy-start | bytes 9220
  63.9 11.3 %slice-start = ((s8[4718592]{0:T(1024)(128)(4,1)}), s8[4194304]{0:T(1024)(128)(4,1)S(1)}, s32[]{:S(2)}) async-start(s8[4718592]{0:T(1024)(128)(4,1)} %bitcast.21), calls=%async_computation.2 | async-start | bytes 8388608
  63.9 11.3 %slice-start.2 = ((s8[4718592]{0:T(1024)(128)(4,1)}), s8[4194304]{0:T(1024)(128)(4,1)S(1)}, s32[]{:S(2)}) async-start(s8[4718592]{0:T(1024)(128)(4,1)} %bitcast.27), calls=%async_computation.4 | async-start | bytes 8388608
  64.3 5.1 %copy-start.5 = (bf16[64,1536]{1,0:T(8,128)(2,1)S(1)}, bf16[64,1536]{1,0:T(8,128)(2,1)}, u32[]{:S(2)}) copy-start(bf16[64,1536]{1,0:T(8,128)(2,1)} %copy-done.4) | copy-start | bytes 589828
  64.3 11.0 %slice-start.1 = ((s8[4718592]{0:T(1024)(128)(4,1)}), s8[524288]{0:T(1024)(128)(4,1)S(1)}, s32[]{:S(2)}) async-start(s8[4718592]{0:T(1024)(128)(4,1)} %bitcast.21), calls=%async_computation.3 | async-start | bytes 1048576
  64.3 11.0 %slice-start.3 = ((s8[4718592]{0:T(1024)(128)(4,1)}), s8[524288]{0:T(1024)(128)(4,1)S(1)}, s32[]{:S(2)}) async-start(s8[4718592]{0:T(1024)(128)(4,1)} %bitcast.27), calls=%async_computation.5 | async-start | bytes 1048576
  67.8 16.0 %collective-permute-start.6 = (bf16[64,1536]{1,0:T(8,128)(2,1)S(1)}, bf16[64,1536]{1,0:T(8,128)(2,1)S(1)}, u32[]{:S(2)}, u32[]{:S(2)}) collective-permute-start(bf16[64,1536]{1,0:T(8,128)(2,1)S(1)} %copy-done.7), channel_id=1, source_target_pairs={{0,2},{2,0},{4,6},{6,4},{8,10},{10,8},{12,14},{14,12},{16,18},{18,... | collective-permute-start | bytes 589832 | tf_op jit(solution)/shard_map/ppermute | solution.py:260
  69.4 14.5 %collective-permute-start.7 = (bf16[64,1536]{1,0:T(8,128)(2,1)S(1)}, bf16[64,1536]{1,0:T(8,128)(2,1)S(1)}, u32[]{:S(2)}, u32[]{:S(2)}) collective-permute-start(bf16[64,1536]{1,0:T(8,128)(2,1)S(1)} %copy-done.5), channel_id=1, source_target_pairs={{0,4},{2,6},{4,0},{6,2},{8,12},{10,14},{12,8},{14,10},{16,20},{18,... | collective-permute-start | bytes 589832 | tf_op jit(solution)/shard_map/ppermute | solution.py:260
  72.8 11.0 %collective-permute-start.8 = (bf16[64,1536]{1,0:T(8,128)(2,1)S(1)}, bf16[64,1536]{1,0:T(8,128)(2,1)S(1)}, u32[]{:S(2)}, u32[]{:S(2)}) collective-permute-start(bf16[64,1536]{1,0:T(8,128)(2,1)S(1)} %get-tuple-element.29), channel_id=1, source_target_pairs={{0,6},{2,4},{4,2},{6,0},{8,14},{10,12},{12,10},{14,8},{16,22},{18,... | collective-permute-start | bytes 589832 | tf_op jit(solution)/shard_map/ppermute | solution.py:260
  75.1 16.5 %collective-permute-start.19 = (bf16[256,1536]{1,0:T(8,128)(2,1)S(1)}, bf16[256,1536]{1,0:T(8,128)(2,1)S(1)}, u32[]{:S(2)}, u32[]{:S(2)}) collective-permute-start(bf16[256,1536]{1,0:T(8,128)(2,1)S(1)} %join.3.own_ref), channel_id=1, source_target_pairs={{0,1},{1,0},{2,3},{3,2},{4,5},{5,4},{6,7},{7,6},{8,9},{9,8},{10,11... | collective-permute-start | bytes 2359304 | tf_op jit(solution)/shard_map/ppermute | solution.py:14
  75.2 8.8 %slice-start.4 = ((s8[4718592]{0:T(1024)(128)(4,1)}), s8[4194304]{0:T(1024)(128)(4,1)S(1)}, s32[]{:S(2)}) async-start(s8[4718592]{0:T(1024)(128)(4,1)} %bitcast.39), calls=%async_computation.6 | async-start | bytes 8388608
  75.3 8.7 %slice-start.5 = ((s8[4718592]{0:T(1024)(128)(4,1)}), s8[524288]{0:T(1024)(128)(4,1)S(1)}, s32[]{:S(2)}) async-start(s8[4718592]{0:T(1024)(128)(4,1)} %bitcast.39), calls=%async_computation.7 | async-start | bytes 1048576
  83.0 3.7 %collective-permute-start.1 = (bf16[512,768]{1,0:T(8,128)(2,1)S(1)}, bf16[512,768]{1,0:T(8,128)(2,1)S(1)}, u32[]{:S(2)}, u32[]{:S(2)}) collective-permute-start(bf16[512,768]{1,0:T(8,128)(2,1)S(1)} %get-tuple-element.25), channel_id=1, source_target_pairs={{0,1},{1,0},{2,3},{3,2},{4,5},{5,4},{6,7},{7,6},{8,9},{9,8},{10,11... | collective-permute-start | bytes 2359304 | tf_op jit(solution)/shard_map/ppermute | solution.py:14
  83.9 16.6 %collective-permute-start.9 = (bf16[256,1536]{1,0:T(8,128)(2,1)S(1)}, bf16[256,1536]{1,0:T(8,128)(2,1)}, u32[]{:S(2)}, u32[]{:S(2)}) collective-permute-start(bf16[256,1536]{1,0:T(8,128)(2,1)S(1)} %join.2.own_ref), channel_id=1, source_target_pairs={{0,1},{1,0},{2,3},{3,2},{4,5},{5,4},{6,7},{7,6},{8,9},{9,8},{10,11... | collective-permute-start | bytes 2359304 | tf_op jit(solution)/shard_map/ppermute | solution.py:14
  86.3 30.6 %collective-permute-start.27 = (bf16[768,256]{0,1:T(8,128)(2,1)}, bf16[768,256]{0,1:T(8,128)(2,1)}, u32[]{:S(2)}, u32[]{:S(2)}) collective-permute-start(bf16[768,256]{0,1:T(8,128)(2,1)} %broadcast_select_fusion.2), channel_id=1, source_target_pairs={{0,1},{1,0},{2,3},{3,2},{4,5},{5,4},{6,7},{7,6},{8,9},{9,8},{10,11... | collective-permute-start | bytes 1179656 | tf_op jit(solution)/shard_map/ppermute | solution.py:14
  87.8 58.6 %all-to-all-start.1 = ((bf16[8,64,768]{2,1,0:T(8,128)(2,1)}), bf16[8,64,768]{2,1,0:T(8,128)(2,1)S(1)}, u32[]{:S(2)}, u32[]{:S(2)}) async-start(bf16[8,64,768]{2,1,0:T(8,128)(2,1)} %bitcast.9), calls=%async_computation.1 | async-start | bytes 1572864 | tf_op jit(solution)/shard_map/all_to_all | solution.py:263
  100.3 6.6 %collective-permute-start.20 = (bf16[256,768]{1,0:T(8,128)(2,1)S(1)}, bf16[256,768]{1,0:T(8,128)(2,1)S(1)}, u32[]{:S(2)}, u32[]{:S(2)}) collective-permute-start(bf16[256,768]{1,0:T(8,128)(2,1)S(1)} %get-tuple-element.41), channel_id=1, source_target_pairs={{0,1},{1,0},{2,3},{3,2},{4,5},{5,4},{6,7},{7,6},{8,9},{9,8},{10,11... | collective-permute-start | bytes 1179656 | tf_op jit(solution)/shard_map/ppermute | solution.py:14
  105.7 30.1 %copy-start.10 = (bf16[1536,256]{0,1:T(8,128)(2,1)S(1)}, bf16[1536,256]{0,1:T(8,128)(2,1)}, u32[]{:S(2)}) copy-start(bf16[1536,256]{0,1:T(8,128)(2,1)} %copy-done.9) | copy-start | bytes 2359300
  105.7 10.6 %collective-permute-start.10 = (bf16[256,768]{1,0:T(8,128)(2,1)S(1)}, bf16[256,768]{1,0:T(8,128)(2,1)S(1)}, u32[]{:S(2)}, u32[]{:S(2)}) collective-permute-start(bf16[256,768]{1,0:T(8,128)(2,1)S(1)} %get-tuple-element.31), channel_id=1, source_target_pairs={{0,1},{1,0},{2,3},{3,2},{4,5},{5,4},{6,7},{7,6},{8,9},{9,8},{10,11... | collective-permute-start | bytes 1179656 | tf_op jit(solution)/shard_map/ppermute | solution.py:14
  107.1 9.9 %collective-permute-start.21 = (bf16[64,768]{1,0:T(8,128)(2,1)S(1)}, bf16[64,768]{1,0:T(8,128)(2,1)S(1)}, u32[]{:S(2)}, u32[]{:S(2)}) collective-permute-start(bf16[64,768]{1,0:T(8,128)(2,1)S(1)} %get-tuple-element.42), channel_id=1, source_target_pairs={{0,24},{2,26},{4,28},{6,30},{8,16},{10,18},{12,20},{14,22},{16,8},... | collective-permute-start | bytes 294920 | tf_op jit(solution)/shard_map/ppermute | solution.py:260
  110.5 18.3 %collective-permute-start.22 = (bf16[64,768]{1,0:T(8,128)(2,1)S(1)}, bf16[64,768]{1,0:T(8,128)(2,1)S(1)}, u32[]{:S(2)}, u32[]{:S(2)}) collective-permute-start(bf16[64,768]{1,0:T(8,128)(2,1)S(1)} %get-tuple-element.43), channel_id=1, source_target_pairs={{0,26},{2,24},{4,30},{6,28},{8,18},{10,16},{12,22},{14,20},{16,10}... | collective-permute-start | bytes 294920 | tf_op jit(solution)/shard_map/ppermute | solution.py:260
  112.1 18.6 %collective-permute-start.23 = (bf16[64,768]{1,0:T(8,128)(2,1)S(1)}, bf16[64,768]{1,0:T(8,128)(2,1)S(1)}, u32[]{:S(2)}, u32[]{:S(2)}) collective-permute-start(bf16[64,768]{1,0:T(8,128)(2,1)S(1)} %get-tuple-element.44), channel_id=1, source_target_pairs={{0,28},{2,30},{4,24},{6,26},{8,20},{10,22},{12,16},{14,18},{16,12}... | collective-permute-start | bytes 294920 | tf_op jit(solution)/shard_map/ppermute | solution.py:260
  116.3 21.5 %collective-permute-start.24 = (bf16[64,768]{1,0:T(8,128)(2,1)S(1)}, bf16[64,768]{1,0:T(8,128)(2,1)S(1)}, u32[]{:S(2)}, u32[]{:S(2)}) collective-permute-start(bf16[64,768]{1,0:T(8,128)(2,1)S(1)} %get-tuple-element.45), channel_id=1, source_target_pairs={{0,30},{2,28},{4,26},{6,24},{8,22},{10,20},{12,18},{14,16},{16,14}... | collective-permute-start | bytes 294920 | tf_op jit(solution)/shard_map/ppermute | solution.py:260
  116.9 22.2 %collective-permute-start.11 = (bf16[64,768]{1,0:T(8,128)(2,1)S(1)}, bf16[64,768]{1,0:T(8,128)(2,1)S(1)}, u32[]{:S(2)}, u32[]{:S(2)}) collective-permute-start(bf16[64,768]{1,0:T(8,128)(2,1)S(1)} %get-tuple-element.32), channel_id=1, source_target_pairs={{0,16},{2,18},{4,20},{6,22},{8,24},{10,26},{12,28},{14,30},{16,0},... | collective-permute-start | bytes 294920 | tf_op jit(solution)/shard_map/ppermute | solution.py:260
  117.0 25.3 %collective-permute-start.12 = (bf16[64,768]{1,0:T(8,128)(2,1)S(1)}, bf16[64,768]{1,0:T(8,128)(2,1)S(1)}, u32[]{:S(2)}, u32[]{:S(2)}) collective-permute-start(bf16[64,768]{1,0:T(8,128)(2,1)S(1)} %get-tuple-element.33), channel_id=1, source_target_pairs={{0,18},{2,16},{4,22},{6,20},{8,26},{10,24},{12,30},{14,28},{16,2},... | collective-permute-start | bytes 294920 | tf_op jit(solution)/shard_map/ppermute | solution.py:260
  128.8 15.6 %collective-permute-start.13 = (bf16[64,768]{1,0:T(8,128)(2,1)S(1)}, bf16[64,768]{1,0:T(8,128)(2,1)S(1)}, u32[]{:S(2)}, u32[]{:S(2)}) collective-permute-start(bf16[64,768]{1,0:T(8,128)(2,1)S(1)} %get-tuple-element.34), channel_id=1, source_target_pairs={{0,20},{2,22},{4,16},{6,18},{8,28},{10,30},{12,24},{14,26},{16,4},... | collective-permute-start | bytes 294920 | tf_op jit(solution)/shard_map/ppermute | solution.py:260
  130.7 15.7 %collective-permute-start.14 = (bf16[64,768]{1,0:T(8,128)(2,1)S(1)}, bf16[64,768]{1,0:T(8,128)(2,1)S(1)}, u32[]{:S(2)}, u32[]{:S(2)}) collective-permute-start(bf16[64,768]{1,0:T(8,128)(2,1)S(1)} %get-tuple-element.35), channel_id=1, source_target_pairs={{0,22},{2,20},{4,18},{6,16},{8,30},{10,28},{12,26},{14,24},{16,6},... | collective-permute-start | bytes 294920 | tf_op jit(solution)/shard_map/ppermute | solution.py:260
  (32 other events, 117.9 us)

commit v3 on v2

--- a/solution.py
+++ b/solution.py
@@ -100,62 +100,65 @@
     return lax.dot_general(a, w, (((1,), (over,)), ((), ())), preferred_element_type=F32)
 
 
-def warm_kernel(in_ref, out_ref, done_ref):
-    done_ref[...] = jnp.zeros_like(done_ref)
-
-
-def warm(w_in, w_out):
-    return pl.pallas_call(
-        warm_kernel,
-        out_shape=jax.ShapeDtypeStruct((8, 128), F32),
-        in_specs=[pl.BlockSpec(memory_space=pltpu.VMEM)] * 2,
-        out_specs=pl.BlockSpec(memory_space=pltpu.VMEM),
-        cost_estimate=pl.CostEstimate(flops=0, bytes_accessed=4096, transcendentals=0),
-        compiler_params=pltpu.CompilerParams(vmem_limit_bytes=1 << 20),
-        name="warm",
-    )(w_in, w_out)
-
-
-def expert_kernel(core_ref, own_ref, oth_ref, in_ref, out_ref, here_ref, away_ref, hidden):
+def expert_kernel(core_ref, own_ref, oth_ref, in_ref, out_ref, here_ref, away_ref, hidden, *held):
     channels = own_ref.shape[1] // 2
     width = in_ref.shape[1]
     chunk = math.gcd(width, 512)
     piece = math.gcd(channels, 256)
     own = pl.multiple_of(core_ref[0] * channels, channels)
     oth = pl.multiple_of((1 - core_ref[0]) * channels, channels)
+    here_in, here_out, sems = held if held else (in_ref, out_ref, None)
+    copies = []
+    for i, at in enumerate(range(0, width, chunk)):
+        part = pl.ds(at, chunk)
+        if held:
+            copies.append(pltpu.make_async_copy(in_ref.at[:, part], here_in.at[:, part], sems.at[0, i]))
+            copies[-1].start()
+            copies.append(pltpu.make_async_copy(out_ref.at[part, :], here_out.at[part, :], sems.at[1, i]))
+            copies[-1].start()
+    copies = iter(copies)
     for at in range(0, width, chunk):
         part = slice(at, at + chunk)
-        one = times(own_ref[:, :channels], in_ref[pl.ds(own, channels), part], 0)
-        one += times(oth_ref[:, :channels], in_ref[pl.ds(oth, channels), part], 0)
-        two = times(own_ref[:, channels:], out_ref[part, pl.ds(own, channels)], 1)
-        two += times(oth_ref[:, channels:], out_ref[part, pl.ds(oth, channels)], 1)
+        if held:
+            next(copies).wait()
+        one = times(own_ref[:, :channels], here_in[pl.ds(own, channels), part], 0)
+        one += times(oth_ref[:, :channels], here_in[pl.ds(oth, channels), part], 0)
+        if held:
+            next(copies).wait()
+        two = times(own_ref[:, channels:], here_out[part, pl.ds(own, channels)], 1)
+        two += times(oth_ref[:, channels:], here_out[part, pl.ds(oth, channels)], 1)
         hidden[:, part] = gradient(one, two)
     for ref, begin in ((away_ref, oth), (here_ref, own)):
         for at in range(0, channels, piece):
             rows = pl.ds(pl.multiple_of(begin + at, piece), piece)
-            ref[:, at : at + piece] = times(hidden[...], in_ref[rows, :], 1).astype(BF)
-
-
-def expert(core, own, oth, w_in, w_out):
+            ref[:, at : at + piece] = times(hidden[...], here_in[rows, :], 1).astype(BF)
+
+
+def expert(core, own, oth, w_in, w_out, fetch):
     rows, channels = own.shape[0], own.shape[1] // 2
     width = w_in.shape[1]
     whole = pl.BlockSpec((rows, 2 * channels), lambda i: (0, 0))
     out = pl.BlockSpec((rows, channels), lambda i: (0, 0))
     shape = jax.ShapeDtypeStruct((rows, channels), BF)
+    weight = pl.BlockSpec(memory_space=pltpu.HBM if fetch else pltpu.VMEM)
+    held = [pltpu.VMEM(w.shape, BF) for w in (w_in, w_out)] + [
+        pltpu.SemaphoreType.DMA((2, width // math.gcd(width, 512)))
+    ]
     return pl.pallas_call(
         expert_kernel,
         grid=(1,),
         out_shape=(shape, shape),
-        in_specs=[pl.BlockSpec(memory_space=pltpu.SMEM), whole, whole]
-        + [pl.BlockSpec(memory_space=pltpu.VMEM)] * 2,
+        in_specs=[pl.BlockSpec(memory_space=pltpu.SMEM), whole, whole, weight, weight],
         out_specs=(out, out),
-        scratch_shapes=[pltpu.VMEM((rows, width), BF)],
+        scratch_shapes=[pltpu.VMEM((rows, width), BF)] + (held if fetch else []),
         cost_estimate=pl.CostEstimate(
             flops=12 * rows * channels * width,
             bytes_accessed=8 * width * channels + 12 * rows * channels,
             transcendentals=rows * width,
         ),
-        compiler_params=pltpu.CompilerParams(vmem_limit_bytes=rows * (8 * width + 24 * channels) + (1 << 20)),
+        compiler_params=pltpu.CompilerParams(
+            vmem_limit_bytes=rows * (8 * width + 24 * channels) + ((11 if rows > 256 else 1) << 20)
+        ),
         name="expert",
     )(core.reshape(1), own, oth, w_in, w_out)
 
@@ -286,12 +289,11 @@
             return jnp.split(part, pieces, axis=0)
         core = lax.axis_index("tensor")
         oth = swap(own)
-        here, away = expert(core, own, oth, w_in, w_out)
+        here, away = expert(core, own, oth, w_in, w_out, False)
         back = swap(away)
         return finish(here, back, pieces)
 
-    ready = warm(w_in, w_out)
-    plane = join(arrived[:quarter], ready)
+    plane = join(arrived[:quarter])
     beyond = join(arrived[quarter:])
     far_grads = list(share(plane, quarter))
     (near_grads,) = share(near_rows, 1)

time: 149 us -> 148 us (level)
  local copies, waits for them, and re-layouts: 23.1 us -> 14 us
  waiting for transfers between devices: 15.3 us -> 20.9 us
  starting transfers between devices: 69.5 us -> 72.9 us
    ppermute x19, waiting for transfers between devices: 15.3 us -> 20.9 us  [flip(): return lax.ppermute(x, 'expert', [(i, i ^ by) for i in range(sources)])]
    unnamed x102 -> x100, local copies, waits for them, and re-layouts: 17.9 us -> 12.6 us
    ppermute x19, starting transfers between devices: 56.2 us -> 59.6 us  [flip(): return lax.ppermute(x, 'expert', [(i, i ^ by) for i in range(sources)])]
    slice x2, local copies, waits for them, and re-layouts: 3.86 us -> 1.45 us  [body(): mix_grad = mix_grad + kernel[offset] * extended[offset:offset + frames]]
  transfers between devices with their start and end apart: 30 -> 30, of which waited for: 6 -> 6; matrix products, arithmetic and copies ran while one was open for 17% -> 14% of each run, Pallas kernels for 13% -> 14%
where the time goes in v3:
time: 148 us; the launch traced here: 147 us
  starting transfers between devices  72.9 us (49%)
  Pallas kernels  24.4 us (16%)
  waiting for transfers between devices  20.9 us (14%)
  local copies, waits for them, and re-layouts  14 us (9%)
  other arithmetic  7.9 us (5%)
  matrix products  5.39 us (4%)
  between operations  1.5 us (1%)
    ppermute x19, starting transfers between devices, flip(): return lax.ppermute(x, 'expert', [(i, i ^ by) for i in range(sources)])  59.6 us
    ppermute x19, waiting for transfers between devices, flip(): return lax.ppermute(x, 'expert', [(i, i ^ by) for i in range(sources)])  20.9 us
    pallas_call x3, Pallas kernels, expert(): pl.pallas_call(expert_kernel, grid=(1,), out_shape=(shape, shape), in_spe...  17.1 us
    unnamed x100, local copies, waits for them, and re-layouts  12.6 us
    all_to_all x2, starting transfers between devices, in_half(): lax.all_to_all(rows, 'expert', split_axis=0, concat_axis=0, tiled=True, a...  10.1 us
    pallas_call x2, Pallas kernels, dispatch(): pl.pallas_call(dispatch_kernel, grid=(1,), out_shape=shape, in_specs=[pl....  4.62 us
    dot_general x1, matrix products, body(): glu_pre = jnp.dot(conv_wide, glu_weight, preferred_element_type=F32)  3.8 us
    another operation x2, other arithmetic  3.75 us
  transfers between devices with their start and end apart: 30, of which 6 were waited for; matrix products, arithmetic and copies ran while one was open for 14% of the time, Pallas kernels for 14%

profile of v3, /device:TPU:0, one launch (start us, length us, event | category | flops | bytes accessed | tf_op | source)
XLA Modules:
  0.0 147.0 jit_solution(8723650401279113641)
XLA Ops:
  0.6 3.1 %dispatch.2 = bf16[8,64,1536]{2,1,0:T(8,128)(2,1)} custom-call(s32[1]{0:T(128)} %bitcast.4.origin_ref, s32[2,256]{1,0:T(2,128)} %bitcast.40, f32[2,256]{1,0:T(2,128)} %bitcast.42, bf16[256,768]{1,0:T(8,128)(2,1)} %in_ref.1, bf16[256,768]{1,0:T(8,128)(2,1)} %grad_ref.1), custom_call_target="tpu_custom_call" | custom-call | flops 402653184 | bytes 2359296 | tf_op jit(solution)/shard_map/dispatch/pallas_call | solution.py:79
  3.7 6.4 %all-to-all-start = ((bf16[8,64,1536]{2,1,0:T(8,128)(2,1)}), bf16[8,64,1536]{2,1,0:T(8,128)(2,1)S(1)}, u32[]{:S(2)}, u32[]{:S(2)}) async-start(bf16[8,64,1536]{2,1,0:T(8,128)(2,1)} %dispatch.2), calls=%async_computation | async-start | bytes 3145728 | tf_op jit(solution)/shard_map/all_to_all | solution.py:266
  10.1 2.7 %collective-permute-start.4 = (bf16[256,768]{1,0:T(8,128)(2,1)S(1)}, bf16[256,768]{1,0:T(8,128)(2,1)S(1)}, u32[]{:S(2)}, u32[]{:S(2)}) collective-permute-start(bf16[256,768]{1,0:T(8,128)(2,1)S(1)} %copy-done.10), channel_id=1, source_target_pairs={{0,16},{2,18},{4,20},{6,22},{8,24},{10,26},{12,28},{14,30},{16,0},... | collective-permute-start | bytes 1179656 | tf_op jit(solution)/shard_map/ppermute | solution.py:263
  13.1 2.6 %collective-permute-start.2 = (s32[256,2]{0,1:T(2,128)S(1)}, s32[256,2]{0,1:T(2,128)S(1)}, u32[]{:S(2)}, u32[]{:S(2)}) collective-permute-start(s32[256,2]{0,1:T(2,128)S(1)} %copy-done.40), channel_id=1, source_target_pairs={{0,16},{2,18},{4,20},{6,22},{8,24},{10,26},{12,28},{14,30},{16,0},... | collective-permute-start | bytes 6152 | tf_op jit(solution)/shard_map/ppermute | solution.py:263
  15.7 1.3 collective-permute-start.25
  17.0 0.8 slice_reduce_fusion.31
  17.7 0.7 slice_reduce_fusion.30
  18.4 5.4 %copy.13 = bf16[192,8,2,768]{3,1,2,0:T(8,128)(2,1)} copy(bf16[192,8,2,768]{3,2,1,0:T(2,128)(2,1)} %bitcast.35) | data formatting | bytes 9437184
  23.8 9.3 %collective-permute-start.3 = (f32[256,2]{0,1:T(2,128)S(1)}, f32[256,2]{0,1:T(2,128)S(1)}, u32[]{:S(2)}, u32[]{:S(2)}) collective-permute-start(f32[256,2]{0,1:T(2,128)S(1)} %copy-done.42), channel_id=1, source_target_pairs={{0,16},{2,18},{4,20},{6,22},{8,24},{10,26},{12,28},{14,30},{16,0},... | collective-permute-start | bytes 6152 | tf_op jit(solution)/shard_map/ppermute | solution.py:263
  33.1 1.0 maximum_convert_fusion
  34.1 10.2 %collective-permute-done.2 = s32[256,2]{0,1:T(2,128)S(1)} collective-permute-done((s32[256,2]{0,1:T(2,128)S(1)}, s32[256,2]{0,1:T(2,128)S(1)}, u32[]{:S(2)}, u32[]{:S(2)}) %collective-permute-start.2) | collective-permute-done | bytes 2080 | tf_op jit(solution)/shard_map/ppermute | solution.py:263
  44.3 1.6 %dispatch.3 = (bf16[64,1536]{1,0:T(8,128)(2,1)S(1)}, bf16[64,1536]{1,0:T(8,128)(2,1)S(1)}, bf16[64,1536]{1,0:T(8,128)(2,1)S(1)}, bf16[64,1536]{1,0:T(8,128)(2,1)...) custom-call(s32[1]{0:T(128)} %bitcast.11.origin_ref, ...), custom_call_target="tpu_custom_call" | custom-call | flops 402653184 | bytes 37748736 | tf_op jit(solution)/shard_map/dispatch/pallas_call | solution.py:79
  45.8 0.7 copy-done.2
  46.5 0.7 copy-done.4
  47.2 7.0 %collective-permute-start.15 = (bf16[64,1536]{1,0:T(8,128)(2,1)}, bf16[64,1536]{1,0:T(8,128)(2,1)S(1)}, u32[]{:S(2)}, u32[]{:S(2)}) collective-permute-start(bf16[64,1536]{1,0:T(8,128)(2,1)} %get-tuple-element.36), channel_id=1, source_target_pairs={{0,8},{2,10},{4,12},{6,14},{8,0},{10,2},{12,4},{14,6},{16,24},{18,... | collective-permute-start | bytes 589832 | tf_op jit(solution)/shard_map/ppermute | solution.py:263
  54.2 4.3 %collective-permute-start.17 = (bf16[64,1536]{1,0:T(8,128)(2,1)}, bf16[64,1536]{1,0:T(8,128)(2,1)S(1)}, u32[]{:S(2)}, u32[]{:S(2)}) collective-permute-start(bf16[64,1536]{1,0:T(8,128)(2,1)} %get-tuple-element.38), channel_id=1, source_target_pairs={{0,12},{2,14},{4,8},{6,10},{8,4},{10,6},{12,0},{14,2},{16,28},{18,... | collective-permute-start | bytes 589832 | tf_op jit(solution)/shard_map/ppermute | solution.py:263
  58.5 1.2 broadcast_select_fusion.1
  60.1 3.8 %fusion.39 = f32[256,1536]{1,0:T(8,128)S(1)} fusion(bf16[1536,1536]{1,0:T(8,128)(2,1)} %bitcast.36, bf16[256,768]{1,0:T(8,128)(2,1)S(1)} %get-tuple-element.83, bf16[256,768]{1,0:T(8,128)(2,1)S(1)} %get-tuple-element.82), kind=kOutput, calls=%fused_computation.75 | convolution fusion | flops 1209532416 | bytes 7077888 | tf_op jit(solution)/shard_map/dot_general | solution.py:312
  64.2 3.5 %multiply_convert_fusion = (bf16[256,768]{1,0:T(8,128)(2,1)S(1)}, f32[256,768]{1,0:T(8,128)S(1)}) fusion(f32[256,1536]{1,0:T(8,128)S(1)} %fusion.39, f32[287,768]{1,0:T(8,128)S(1)} %copy-done.6, f32[768]{0:T(1024)S(1)} %copy-done.38, f32[768]{0:T(1024)S(1)} %copy-done.39, f32[768]{0:T(1024)S(1)} %get-tuple-element.49, f32[768]{0:T(1024)S(1)} %get-tuple-element.50, ...), kind=kLoop, calls=%fused_computation.83 | loop fusion | flops 13369344 | bytes 27230208 | tf_op jit(solution)/shard_map/convert
  67.8 1.5 %collective-permute-start.6 = (bf16[64,1536]{1,0:T(8,128)(2,1)S(1)}, bf16[64,1536]{1,0:T(8,128)(2,1)S(1)}, u32[]{:S(2)}, u32[]{:S(2)}) collective-permute-start(bf16[64,1536]{1,0:T(8,128)(2,1)S(1)} %copy-done.5), channel_id=1, source_target_pairs={{0,2},{2,0},{4,6},{6,4},{8,10},{10,8},{12,14},{14,12},{16,18},{18,... | collective-permute-start | bytes 589832 | tf_op jit(solution)/shard_map/ppermute | solution.py:263
  69.3 3.5 %collective-permute-start.7 = (bf16[64,1536]{1,0:T(8,128)(2,1)S(1)}, bf16[64,1536]{1,0:T(8,128)(2,1)S(1)}, u32[]{:S(2)}, u32[]{:S(2)}) collective-permute-start(bf16[64,1536]{1,0:T(8,128)(2,1)S(1)} %copy-done.3), channel_id=1, source_target_pairs={{0,4},{2,6},{4,0},{6,2},{8,12},{10,14},{12,8},{14,10},{16,20},{18,... | collective-permute-start | bytes 589832 | tf_op jit(solution)/shard_map/ppermute | solution.py:263
  72.8 2.1 %collective-permute-done.18.refs_3_ = bf16[64,1536]{1,0:T(8,128)(2,1)S(1)} collective-permute-done((bf16[64,1536]{1,0:T(8,128)(2,1)}, bf16[64,1536]{1,0:T(8,128)(2,1)S(1)}, u32[]{:S(2)}, u32[]{:S(2)}) %collective-permute-start.18) | collective-permute-done | bytes 196640 | tf_op jit(solution)/shard_map/ppermute | solution.py:263
  75.1 7.9 %expert.3 = (bf16[512,768]{1,0:T(8,128)(2,1)S(1)}, bf16[512,768]{1,0:T(8,128)(2,1)S(1)}) custom-call(s32[1]{0:T(128)} %bitcast.3.core_ref, bf16[512,1536]{1,0:T(8,128)(2,1)S(1)} %bitcast.22, bf16[512,1536]{1,0:T(8,128)(2,1)S(1)} %collective-permute-done.oth_ref, bf16[1536,1536]{1,0:T(8,128)(2,1)S(1)} %bitcast.25, bf16[1536,1536]{1,0:T(8,128)(2,1)S(1)} %bitcast.30), custom_call_target="tpu_custom_call" | custom-call | flops 7247757312 | bytes 14155776 | tf_op jit(solution)/shard_map/expert/pallas_call | solution.py:147
  83.0 0.5 collective-permute-start.1
  84.0 1.4 fusion
  85.4 0.8 broadcast_select_fusion.2
  86.3 0.5 collective-permute-start.27
  86.7 1.1 finish.3
  87.8 3.8 %all-to-all-start.1 = ((bf16[8,64,768]{2,1,0:T(8,128)(2,1)}), bf16[8,64,768]{2,1,0:T(8,128)(2,1)S(1)}, u32[]{:S(2)}, u32[]{:S(2)}) async-start(bf16[8,64,768]{2,1,0:T(8,128)(2,1)} %bitcast.9), calls=%async_computation.1 | async-start | bytes 1572864 | tf_op jit(solution)/shard_map/all_to_all | solution.py:266
  91.6 2.3 %copy-done = bf16[1,1536,1536]{2,1,0:T(8,128)(2,1)S(1)} copy-done((bf16[1,1536,1536]{2,1,0:T(8,128)(2,1)S(1)}, bf16[1,1536,1536]{2,1,0:T(8,128)(2,1)}, u32[]{:S(2)}) %copy-start) | copy-done | bytes 4718616
  93.9 2.3 %copy-done.1 = bf16[1,1536,1536]{2,1,0:T(8,128)(2,1)S(1)} copy-done((bf16[1,1536,1536]{2,1,0:T(8,128)(2,1)S(1)}, bf16[1,1536,1536]{2,1,0:T(8,128)(2,1)}, u32[]{:S(2)}) %copy-start.1) | copy-done | bytes 4718616
  96.3 4.0 %expert.5 = (bf16[256,768]{1,0:T(8,128)(2,1)S(1)}, bf16[256,768]{1,0:T(8,128)(2,1)S(1)}) custom-call(s32[1]{0:T(128)} %bitcast.3.core_ref, bf16[256,1536]{1,0:T(8,128)(2,1)S(1)} %join.3.own_ref, bf16[256,1536]{1,0:T(8,128)(2,1)S(1)} %collective-permute-done.19.oth_ref, bf16[1536,1536]{1,0:T(8,128)(2,1)S(1)} %bitcast.26, bf16[1536,1536]{1,0:T(8,128)(2,1)S(1)} %bitcast.31), custom_call_target="tpu_custom_call" | custom-call | flops 3623878656 | bytes 11796480 | tf_op jit(solution)/shard_map/expert/pallas_call | solution.py:147
  100.4 5.2 %expert.4 = (bf16[256,768]{1,0:T(8,128)(2,1)S(1)}, bf16[256,768]{1,0:T(8,128)(2,1)S(1)}) custom-call(s32[1]{0:T(128)} %bitcast.3.core_ref, bf16[256,1536]{1,0:T(8,128)(2,1)S(1)} %join.2.own_ref, bf16[256,1536]{1,0:T(8,128)(2,1)} %collective-permute-done.9.oth_ref, bf16[1536,1536]{1,0:T(8,128)(2,1)S(1)} %bitcast.27, bf16[1536,1536]{1,0:T(8,128)(2,1)S(1)} %bitcast.32), custom_call_target="tpu_custom_call" | custom-call | flops 3623878656 | bytes 11796480 | tf_op jit(solution)/shard_map/expert/pallas_call | solution.py:147
  105.6 0.5 collective-permute-start.10
  106.3 3.4 %collective-permute-start.21 = (bf16[64,768]{1,0:T(8,128)(2,1)S(1)}, bf16[64,768]{1,0:T(8,128)(2,1)S(1)}, u32[]{:S(2)}, u32[]{:S(2)}) collective-permute-start(bf16[64,768]{1,0:T(8,128)(2,1)S(1)} %get-tuple-element.42), channel_id=1, source_target_pairs={{0,24},{2,26},{4,28},{6,30},{8,16},{10,18},{12,20},{14,22},{16,8},... | collective-permute-start | bytes 294920 | tf_op jit(solution)/shard_map/ppermute | solution.py:263
  109.7 1.6 %collective-permute-start.22 = (bf16[64,768]{1,0:T(8,128)(2,1)S(1)}, bf16[64,768]{1,0:T(8,128)(2,1)S(1)}, u32[]{:S(2)}, u32[]{:S(2)}) collective-permute-start(bf16[64,768]{1,0:T(8,128)(2,1)S(1)} %get-tuple-element.43), channel_id=1, source_target_pairs={{0,26},{2,24},{4,30},{6,28},{8,18},{10,16},{12,22},{14,20},{16,10}... | collective-permute-start | bytes 294920 | tf_op jit(solution)/shard_map/ppermute | solution.py:263
  111.3 4.1 %collective-permute-start.23 = (bf16[64,768]{1,0:T(8,128)(2,1)S(1)}, bf16[64,768]{1,0:T(8,128)(2,1)S(1)}, u32[]{:S(2)}, u32[]{:S(2)}) collective-permute-start(bf16[64,768]{1,0:T(8,128)(2,1)S(1)} %get-tuple-element.44), channel_id=1, source_target_pairs={{0,28},{2,30},{4,24},{6,26},{8,20},{10,22},{12,16},{14,18},{16,12}... | collective-permute-start | bytes 294920 | tf_op jit(solution)/shard_map/ppermute | solution.py:263
  115.6 0.5 collective-permute-start.24
  116.2 11.8 %collective-permute-start.12 = (bf16[64,768]{1,0:T(8,128)(2,1)S(1)}, bf16[64,768]{1,0:T(8,128)(2,1)S(1)}, u32[]{:S(2)}, u32[]{:S(2)}) collective-permute-start(bf16[64,768]{1,0:T(8,128)(2,1)S(1)} %get-tuple-element.33), channel_id=1, source_target_pairs={{0,18},{2,16},{4,22},{6,20},{8,26},{10,24},{12,30},{14,28},{16,2},... | collective-permute-start | bytes 294920 | tf_op jit(solution)/shard_map/ppermute | solution.py:263
  128.0 2.0 %collective-permute-start.13 = (bf16[64,768]{1,0:T(8,128)(2,1)S(1)}, bf16[64,768]{1,0:T(8,128)(2,1)S(1)}, u32[]{:S(2)}, u32[]{:S(2)}) collective-permute-start(bf16[64,768]{1,0:T(8,128)(2,1)S(1)} %get-tuple-element.34), channel_id=1, source_target_pairs={{0,20},{2,22},{4,16},{6,18},{8,28},{10,30},{12,24},{14,26},{16,4},... | collective-permute-start | bytes 294920 | tf_op jit(solution)/shard_map/ppermute | solution.py:263
  130.0 5.1 %collective-permute-start.14 = (bf16[64,768]{1,0:T(8,128)(2,1)S(1)}, bf16[64,768]{1,0:T(8,128)(2,1)S(1)}, u32[]{:S(2)}, u32[]{:S(2)}) collective-permute-start(bf16[64,768]{1,0:T(8,128)(2,1)S(1)} %get-tuple-element.35), channel_id=1, source_target_pairs={{0,22},{2,20},{4,18},{6,16},{8,30},{10,28},{12,26},{14,24},{16,6},... | collective-permute-start | bytes 294920 | tf_op jit(solution)/shard_map/ppermute | solution.py:263
  135.1 1.2 add_convert_fusion
  136.2 0.9 copy.12
  137.1 1.1 collective-permute-done.11.refs_0_
  138.3 3.2 %collective-permute-done.12.refs_1_ = bf16[64,768]{1,0:T(8,128)(2,1)S(1)} collective-permute-done((bf16[64,768]{1,0:T(8,128)(2,1)S(1)}, bf16[64,768]{1,0:T(8,128)(2,1)S(1)}, u32[]{:S(2)}, u32[]{:S(2)}) %collective-permute-start.12) | collective-permute-done | bytes 98336 | tf_op jit(solution)/shard_map/ppermute | solution.py:263
  141.5 2.1 %collective-permute-done.13.refs_2_ = bf16[64,768]{1,0:T(8,128)(2,1)S(1)} collective-permute-done((bf16[64,768]{1,0:T(8,128)(2,1)S(1)}, bf16[64,768]{1,0:T(8,128)(2,1)S(1)}, u32[]{:S(2)}, u32[]{:S(2)}) %collective-permute-start.13) | collective-permute-done | bytes 98336 | tf_op jit(solution)/shard_map/ppermute | solution.py:263
  143.6 2.1 %collective-permute-done.14.refs_3_ = bf16[64,768]{1,0:T(8,128)(2,1)S(1)} collective-permute-done((bf16[64,768]{1,0:T(8,128)(2,1)S(1)}, bf16[64,768]{1,0:T(8,128)(2,1)S(1)}, u32[]{:S(2)}, u32[]{:S(2)}) %collective-permute-start.14) | collective-permute-done | bytes 98336 | tf_op jit(solution)/shard_map/ppermute | solution.py:263
  145.7 1.4 combine.1
  (140 shorter events, 1.8 us)
Async XLA Ops:
  3.7 6.4 %copy-start.10 = (bf16[256,768]{1,0:T(8,128)(2,1)S(1)}, bf16[256,768]{1,0:T(8,128)(2,1)}, u32[]{:S(2)}) copy-start(bf16[256,768]{1,0:T(8,128)(2,1)} %in_ref.1) | copy-start | bytes 1179652
  3.7 9.4 %copy-start.40 = (s32[256,2]{0,1:T(2,128)S(1)}, s32[256,2]{0,1:T(2,128)}, u32[]{:S(2)}) copy-start(s32[256,2]{0,1:T(2,128)} %param.12) | copy-start | bytes 6148
  3.7 12.0 %copy-start.9 = (bf16[256,768]{1,0:T(8,128)(2,1)S(1)}, bf16[256,768]{1,0:T(8,128)(2,1)}, u32[]{:S(2)}) copy-start(bf16[256,768]{1,0:T(8,128)(2,1)} %param.19) | copy-start | bytes 1179652
  3.7 13.3 %copy-start.11 = (f32[32,768]{1,0:T(8,128)S(1)}, f32[32,768]{1,0:T(8,128)}, u32[]{:S(2)}) copy-start(f32[32,768]{1,0:T(8,128)} %param.18) | copy-start | bytes 294916
  3.7 56.0 %all-to-all-start = ((bf16[8,64,1536]{2,1,0:T(8,128)(2,1)}), bf16[8,64,1536]{2,1,0:T(8,128)(2,1)S(1)}, u32[]{:S(2)}, u32[]{:S(2)}) async-start(bf16[8,64,1536]{2,1,0:T(8,128)(2,1)} %dispatch.2), calls=%async_computation | async-start | bytes 3145728 | tf_op jit(solution)/shard_map/all_to_all | solution.py:266
  10.1 34.2 %collective-permute-start.4 = (bf16[256,768]{1,0:T(8,128)(2,1)S(1)}, bf16[256,768]{1,0:T(8,128)(2,1)S(1)}, u32[]{:S(2)}, u32[]{:S(2)}) collective-permute-start(bf16[256,768]{1,0:T(8,128)(2,1)S(1)} %copy-done.10), channel_id=1, source_target_pairs={{0,16},{2,18},{4,20},{6,22},{8,24},{10,26},{12,28},{14,30},{16,0},... | collective-permute-start | bytes 1179656 | tf_op jit(solution)/shard_map/ppermute | solution.py:263
  12.7 31.5 %collective-permute-start.5 = (bf16[256,768]{1,0:T(8,128)(2,1)}, bf16[256,768]{1,0:T(8,128)(2,1)S(1)}, u32[]{:S(2)}, u32[]{:S(2)}) collective-permute-start(bf16[256,768]{1,0:T(8,128)(2,1)} %grad_ref.1), channel_id=1, source_target_pairs={{0,16},{2,18},{4,20},{6,22},{8,24},{10,26},{12,28},{14,30},{16,0},... | collective-permute-start | bytes 1179656 | tf_op jit(solution)/shard_map/ppermute | solution.py:263
  13.1 31.2 %collective-permute-start.2 = (s32[256,2]{0,1:T(2,128)S(1)}, s32[256,2]{0,1:T(2,128)S(1)}, u32[]{:S(2)}, u32[]{:S(2)}) collective-permute-start(s32[256,2]{0,1:T(2,128)S(1)} %copy-done.40), channel_id=1, source_target_pairs={{0,16},{2,18},{4,20},{6,22},{8,24},{10,26},{12,28},{14,30},{16,0},... | collective-permute-start | bytes 6152 | tf_op jit(solution)/shard_map/ppermute | solution.py:263
  15.7 42.9 %collective-permute-start.26 = (bf16[256,768]{1,0:T(8,128)(2,1)}, bf16[256,768]{1,0:T(8,128)(2,1)}, u32[]{:S(2)}, u32[]{:S(2)}) collective-permute-start(bf16[256,768]{1,0:T(8,128)(2,1)} %param.16), channel_id=1, source_target_pairs={{0,1},{1,0},{2,3},{3,2},{4,5},{5,4},{6,7},{7,6},{8,9},{9,8},{10,11... | collective-permute-start | bytes 1179656 | tf_op jit(solution)/shard_map/ppermute | solution.py:14
  15.7 8.2 %collective-permute-start.25 = (bf16[31,768]{1,0:T(8,128)(2,1)S(1)}, bf16[31,768]{1,0:T(8,128)(2,1)S(1)}, u32[]{:S(2)}, u32[]{:S(2)}) collective-permute-start(bf16[31,768]{1,0:T(8,128)(2,1)S(1)} %slice.210), channel_id=1, source_target_pairs={{2,0},{4,2},{6,4},{8,6},{10,8},{12,10},{14,12},{16,14},{18,16},{20... | collective-permute-start | bytes 142856 | tf_op jit(solution)/shard_map/ppermute | solution.py:314
  18.4 5.4 %copy-start.42 = (f32[256,2]{0,1:T(2,128)S(1)}, f32[256,2]{0,1:T(2,128)}, u32[]{:S(2)}) copy-start(f32[256,2]{0,1:T(2,128)} %param.13) | copy-start | bytes 6148
  23.8 20.4 %collective-permute-start.3 = (f32[256,2]{0,1:T(2,128)S(1)}, f32[256,2]{0,1:T(2,128)S(1)}, u32[]{:S(2)}, u32[]{:S(2)}) collective-permute-start(f32[256,2]{0,1:T(2,128)S(1)} %copy-done.42), channel_id=1, source_target_pairs={{0,16},{2,18},{4,20},{6,22},{8,24},{10,26},{12,28},{14,30},{16,0},... | collective-permute-start | bytes 6152 | tf_op jit(solution)/shard_map/ppermute | solution.py:263
  47.2 20.6 %collective-permute-start.15 = (bf16[64,1536]{1,0:T(8,128)(2,1)}, bf16[64,1536]{1,0:T(8,128)(2,1)S(1)}, u32[]{:S(2)}, u32[]{:S(2)}) collective-permute-start(bf16[64,1536]{1,0:T(8,128)(2,1)} %get-tuple-element.36), channel_id=1, source_target_pairs={{0,8},{2,10},{4,12},{6,14},{8,0},{10,2},{12,4},{14,6},{16,24},{18,... | collective-permute-start | bytes 589832 | tf_op jit(solution)/shard_map/ppermute | solution.py:263
  54.2 15.1 %collective-permute-start.16 = (bf16[64,1536]{1,0:T(8,128)(2,1)}, bf16[64,1536]{1,0:T(8,128)(2,1)S(1)}, u32[]{:S(2)}, u32[]{:S(2)}) collective-permute-start(bf16[64,1536]{1,0:T(8,128)(2,1)} %get-tuple-element.37), channel_id=1, source_target_pairs={{0,10},{2,8},{4,14},{6,12},{8,2},{10,0},{12,6},{14,4},{16,26},{18,... | collective-permute-start | bytes 589832 | tf_op jit(solution)/shard_map/ppermute | solution.py:263
  54.2 18.6 %collective-permute-start.17 = (bf16[64,1536]{1,0:T(8,128)(2,1)}, bf16[64,1536]{1,0:T(8,128)(2,1)S(1)}, u32[]{:S(2)}, u32[]{:S(2)}) collective-permute-start(bf16[64,1536]{1,0:T(8,128)(2,1)} %get-tuple-element.38), channel_id=1, source_target_pairs={{0,12},{2,14},{4,8},{6,10},{8,4},{10,6},{12,0},{14,2},{16,28},{18,... | collective-permute-start | bytes 589832 | tf_op jit(solution)/shard_map/ppermute | solution.py:263
  58.5 16.4 %collective-permute-start.18 = (bf16[64,1536]{1,0:T(8,128)(2,1)}, bf16[64,1536]{1,0:T(8,128)(2,1)S(1)}, u32[]{:S(2)}, u32[]{:S(2)}) collective-permute-start(bf16[64,1536]{1,0:T(8,128)(2,1)} %get-tuple-element.39), channel_id=1, source_target_pairs={{0,14},{2,12},{4,10},{6,8},{8,6},{10,4},{12,2},{14,0},{16,30},{18,... | collective-permute-start | bytes 589832 | tf_op jit(solution)/shard_map/ppermute | solution.py:263
  59.7 15.4 %collective-permute-start = (bf16[512,1536]{1,0:T(8,128)(2,1)S(1)}, bf16[512,1536]{1,0:T(8,128)(2,1)S(1)}, u32[]{:S(2)}, u32[]{:S(2)}) collective-permute-start(bf16[512,1536]{1,0:T(8,128)(2,1)S(1)} %bitcast.21), channel_id=1, source_target_pairs={{0,1},{1,0},{2,3},{3,2},{4,5},{5,4},{6,7},{7,6},{8,9},{9,8},{10,11... | collective-permute-start | bytes 4718600 | tf_op jit(solution)/shard_map/ppermute | solution.py:14
  59.8 4.1 %copy-start.6 = (f32[287,768]{1,0:T(8,128)S(1)}, f32[287,768]{1,0:T(8,128)}, u32[]{:S(2)}) copy-start(f32[287,768]{1,0:T(8,128)} %maximum_convert_fusion) | copy-start | bytes 2644996
  59.8 4.1 %copy-start.12 = (f32[768]{0:T(1024)S(1)}, f32[768]{0:T(1024)}, u32[]{:S(2)}) copy-start(f32[768]{0:T(1024)} %get-tuple-element.52) | copy-start | bytes 9220
  59.8 4.1 %copy-start.13 = (f32[768]{0:T(1024)S(1)}, f32[768]{0:T(1024)}, u32[]{:S(2)}) copy-start(f32[768]{0:T(1024)} %get-tuple-element.53) | copy-start | bytes 9220
  59.8 4.1 %copy-start.14 = (f32[768]{0:T(1024)S(1)}, f32[768]{0:T(1024)}, u32[]{:S(2)}) copy-start(f32[768]{0:T(1024)} %get-tuple-element.54) | copy-start | bytes 9220
  63.9 11.2 %slice-start = ((s8[4718592]{0:T(1024)(128)(4,1)}), s8[4194304]{0:T(1024)(128)(4,1)S(1)}, s32[]{:S(2)}) async-start(s8[4718592]{0:T(1024)(128)(4,1)} %bitcast.23), calls=%async_computation.2 | async-start | bytes 8388608
  63.9 11.2 %slice-start.2 = ((s8[4718592]{0:T(1024)(128)(4,1)}), s8[4194304]{0:T(1024)(128)(4,1)S(1)}, s32[]{:S(2)}) async-start(s8[4718592]{0:T(1024)(128)(4,1)} %bitcast.28), calls=%async_computation.4 | async-start | bytes 8388608
  64.2 5.1 %copy-start.3 = (bf16[64,1536]{1,0:T(8,128)(2,1)S(1)}, bf16[64,1536]{1,0:T(8,128)(2,1)}, u32[]{:S(2)}) copy-start(bf16[64,1536]{1,0:T(8,128)(2,1)} %copy-done.2) | copy-start | bytes 589828
  64.2 10.9 %slice-start.1 = ((s8[4718592]{0:T(1024)(128)(4,1)}), s8[524288]{0:T(1024)(128)(4,1)S(1)}, s32[]{:S(2)}) async-start(s8[4718592]{0:T(1024)(128)(4,1)} %bitcast.23), calls=%async_computation.3 | async-start | bytes 1048576
  64.2 10.9 %slice-start.3 = ((s8[4718592]{0:T(1024)(128)(4,1)}), s8[524288]{0:T(1024)(128)(4,1)S(1)}, s32[]{:S(2)}) async-start(s8[4718592]{0:T(1024)(128)(4,1)} %bitcast.28), calls=%async_computation.5 | async-start | bytes 1048576
  67.8 16.0 %collective-permute-start.6 = (bf16[64,1536]{1,0:T(8,128)(2,1)S(1)}, bf16[64,1536]{1,0:T(8,128)(2,1)S(1)}, u32[]{:S(2)}, u32[]{:S(2)}) collective-permute-start(bf16[64,1536]{1,0:T(8,128)(2,1)S(1)} %copy-done.5), channel_id=1, source_target_pairs={{0,2},{2,0},{4,6},{6,4},{8,10},{10,8},{12,14},{14,12},{16,18},{18,... | collective-permute-start | bytes 589832 | tf_op jit(solution)/shard_map/ppermute | solution.py:263
  69.3 14.5 %collective-permute-start.7 = (bf16[64,1536]{1,0:T(8,128)(2,1)S(1)}, bf16[64,1536]{1,0:T(8,128)(2,1)S(1)}, u32[]{:S(2)}, u32[]{:S(2)}) collective-permute-start(bf16[64,1536]{1,0:T(8,128)(2,1)S(1)} %copy-done.3), channel_id=1, source_target_pairs={{0,4},{2,6},{4,0},{6,2},{8,12},{10,14},{12,8},{14,10},{16,20},{18,... | collective-permute-start | bytes 589832 | tf_op jit(solution)/shard_map/ppermute | solution.py:263
  72.8 11.0 %collective-permute-start.8 = (bf16[64,1536]{1,0:T(8,128)(2,1)S(1)}, bf16[64,1536]{1,0:T(8,128)(2,1)S(1)}, u32[]{:S(2)}, u32[]{:S(2)}) collective-permute-start(bf16[64,1536]{1,0:T(8,128)(2,1)S(1)} %get-tuple-element.29), channel_id=1, source_target_pairs={{0,6},{2,4},{4,2},{6,0},{8,14},{10,12},{12,10},{14,8},{16,22},{18,... | collective-permute-start | bytes 589832 | tf_op jit(solution)/shard_map/ppermute | solution.py:263
  75.0 16.6 %collective-permute-start.19 = (bf16[256,1536]{1,0:T(8,128)(2,1)S(1)}, bf16[256,1536]{1,0:T(8,128)(2,1)S(1)}, u32[]{:S(2)}, u32[]{:S(2)}) collective-permute-start(bf16[256,1536]{1,0:T(8,128)(2,1)S(1)} %join.3.own_ref), channel_id=1, source_target_pairs={{0,1},{1,0},{2,3},{3,2},{4,5},{5,4},{6,7},{7,6},{8,9},{9,8},{10,11... | collective-permute-start | bytes 2359304 | tf_op jit(solution)/shard_map/ppermute | solution.py:14
  75.1 8.9 %slice-start.4 = ((s8[4718592]{0:T(1024)(128)(4,1)}), s8[4194304]{0:T(1024)(128)(4,1)S(1)}, s32[]{:S(2)}) async-start(s8[4718592]{0:T(1024)(128)(4,1)} %bitcast.37), calls=%async_computation.6 | async-start | bytes 8388608
  75.1 8.8 %slice-start.5 = ((s8[4718592]{0:T(1024)(128)(4,1)}), s8[524288]{0:T(1024)(128)(4,1)S(1)}, s32[]{:S(2)}) async-start(s8[4718592]{0:T(1024)(128)(4,1)} %bitcast.37), calls=%async_computation.7 | async-start | bytes 1048576
  83.0 3.7 %collective-permute-start.1 = (bf16[512,768]{1,0:T(8,128)(2,1)S(1)}, bf16[512,768]{1,0:T(8,128)(2,1)S(1)}, u32[]{:S(2)}, u32[]{:S(2)}) collective-permute-start(bf16[512,768]{1,0:T(8,128)(2,1)S(1)} %get-tuple-element.25), channel_id=1, source_target_pairs={{0,1},{1,0},{2,3},{3,2},{4,5},{5,4},{6,7},{7,6},{8,9},{9,8},{10,11... | collective-permute-start | bytes 2359304 | tf_op jit(solution)/shard_map/ppermute | solution.py:14
  83.9 16.6 %collective-permute-start.9 = (bf16[256,1536]{1,0:T(8,128)(2,1)S(1)}, bf16[256,1536]{1,0:T(8,128)(2,1)}, u32[]{:S(2)}, u32[]{:S(2)}) collective-permute-start(bf16[256,1536]{1,0:T(8,128)(2,1)S(1)} %join.2.own_ref), channel_id=1, source_target_pairs={{0,1},{1,0},{2,3},{3,2},{4,5},{5,4},{6,7},{7,6},{8,9},{9,8},{10,11... | collective-permute-start | bytes 2359304 | tf_op jit(solution)/shard_map/ppermute | solution.py:14
  86.3 29.9 %collective-permute-start.27 = (bf16[768,256]{0,1:T(8,128)(2,1)}, bf16[768,256]{0,1:T(8,128)(2,1)}, u32[]{:S(2)}, u32[]{:S(2)}) collective-permute-start(bf16[768,256]{0,1:T(8,128)(2,1)} %broadcast_select_fusion.2), channel_id=1, source_target_pairs={{0,1},{1,0},{2,3},{3,2},{4,5},{5,4},{6,7},{7,6},{8,9},{9,8},{10,11... | collective-permute-start | bytes 1179656 | tf_op jit(solution)/shard_map/ppermute | solution.py:14
  87.8 57.9 %all-to-all-start.1 = ((bf16[8,64,768]{2,1,0:T(8,128)(2,1)}), bf16[8,64,768]{2,1,0:T(8,128)(2,1)S(1)}, u32[]{:S(2)}, u32[]{:S(2)}) async-start(bf16[8,64,768]{2,1,0:T(8,128)(2,1)} %bitcast.9), calls=%async_computation.1 | async-start | bytes 1572864 | tf_op jit(solution)/shard_map/all_to_all | solution.py:266
  100.3 5.9 %copy-start.41 = (s32[256,2]{0,1:T(2,128)S(1)}, s32[256,2]{0,1:T(2,128)}, u32[]{:S(2)}) copy-start(s32[256,2]{0,1:T(2,128)} %param.12) | copy-start | bytes 6148
  100.3 5.9 %collective-permute-start.20 = (bf16[256,768]{1,0:T(8,128)(2,1)S(1)}, bf16[256,768]{1,0:T(8,128)(2,1)S(1)}, u32[]{:S(2)}, u32[]{:S(2)}) collective-permute-start(bf16[256,768]{1,0:T(8,128)(2,1)S(1)} %get-tuple-element.41), channel_id=1, source_target_pairs={{0,1},{1,0},{2,3},{3,2},{4,5},{5,4},{6,7},{7,6},{8,9},{9,8},{10,11... | collective-permute-start | bytes 1179656 | tf_op jit(solution)/shard_map/ppermute | solution.py:14
  105.6 29.4 %copy-start.8 = (bf16[1536,256]{0,1:T(8,128)(2,1)S(1)}, bf16[1536,256]{0,1:T(8,128)(2,1)}, u32[]{:S(2)}) copy-start(bf16[1536,256]{0,1:T(8,128)(2,1)} %copy-done.7) | copy-start | bytes 2359300
  105.6 9.9 %collective-permute-start.10 = (bf16[256,768]{1,0:T(8,128)(2,1)S(1)}, bf16[256,768]{1,0:T(8,128)(2,1)S(1)}, u32[]{:S(2)}, u32[]{:S(2)}) collective-permute-start(bf16[256,768]{1,0:T(8,128)(2,1)S(1)} %get-tuple-element.31), channel_id=1, source_target_pairs={{0,1},{1,0},{2,3},{3,2},{4,5},{5,4},{6,7},{7,6},{8,9},{9,8},{10,11... | collective-permute-start | bytes 1179656 | tf_op jit(solution)/shard_map/ppermute | solution.py:14
  106.3 9.9 %collective-permute-start.21 = (bf16[64,768]{1,0:T(8,128)(2,1)S(1)}, bf16[64,768]{1,0:T(8,128)(2,1)S(1)}, u32[]{:S(2)}, u32[]{:S(2)}) collective-permute-start(bf16[64,768]{1,0:T(8,128)(2,1)S(1)} %get-tuple-element.42), channel_id=1, source_target_pairs={{0,24},{2,26},{4,28},{6,30},{8,16},{10,18},{12,20},{14,22},{16,8},... | collective-permute-start | bytes 294920 | tf_op jit(solution)/shard_map/ppermute | solution.py:263
  109.7 18.3 %collective-permute-start.22 = (bf16[64,768]{1,0:T(8,128)(2,1)S(1)}, bf16[64,768]{1,0:T(8,128)(2,1)S(1)}, u32[]{:S(2)}, u32[]{:S(2)}) collective-permute-start(bf16[64,768]{1,0:T(8,128)(2,1)S(1)} %get-tuple-element.43), channel_id=1, source_target_pairs={{0,26},{2,24},{4,30},{6,28},{8,18},{10,16},{12,22},{14,20},{16,10}... | collective-permute-start | bytes 294920 | tf_op jit(solution)/shard_map/ppermute | solution.py:263
  111.3 18.7 %collective-permute-start.23 = (bf16[64,768]{1,0:T(8,128)(2,1)S(1)}, bf16[64,768]{1,0:T(8,128)(2,1)S(1)}, u32[]{:S(2)}, u32[]{:S(2)}) collective-permute-start(bf16[64,768]{1,0:T(8,128)(2,1)S(1)} %get-tuple-element.44), channel_id=1, source_target_pairs={{0,28},{2,30},{4,24},{6,26},{8,20},{10,22},{12,16},{14,18},{16,12}... | collective-permute-start | bytes 294920 | tf_op jit(solution)/shard_map/ppermute | solution.py:263
  115.6 21.6 %collective-permute-start.24 = (bf16[64,768]{1,0:T(8,128)(2,1)S(1)}, bf16[64,768]{1,0:T(8,128)(2,1)S(1)}, u32[]{:S(2)}, u32[]{:S(2)}) collective-permute-start(bf16[64,768]{1,0:T(8,128)(2,1)S(1)} %get-tuple-element.45), channel_id=1, source_target_pairs={{0,30},{2,28},{4,26},{6,24},{8,22},{10,20},{12,18},{14,16},{16,14}... | collective-permute-start | bytes 294920 | tf_op jit(solution)/shard_map/ppermute | solution.py:263
  116.1 22.2 %collective-permute-start.11 = (bf16[64,768]{1,0:T(8,128)(2,1)S(1)}, bf16[64,768]{1,0:T(8,128)(2,1)S(1)}, u32[]{:S(2)}, u32[]{:S(2)}) collective-permute-start(bf16[64,768]{1,0:T(8,128)(2,1)S(1)} %get-tuple-element.32), channel_id=1, source_target_pairs={{0,16},{2,18},{4,20},{6,22},{8,24},{10,26},{12,28},{14,30},{16,0},... | collective-permute-start | bytes 294920 | tf_op jit(solution)/shard_map/ppermute | solution.py:263
  116.2 25.3 %collective-permute-start.12 = (bf16[64,768]{1,0:T(8,128)(2,1)S(1)}, bf16[64,768]{1,0:T(8,128)(2,1)S(1)}, u32[]{:S(2)}, u32[]{:S(2)}) collective-permute-start(bf16[64,768]{1,0:T(8,128)(2,1)S(1)} %get-tuple-element.33), channel_id=1, source_target_pairs={{0,18},{2,16},{4,22},{6,20},{8,26},{10,24},{12,30},{14,28},{16,2},... | collective-permute-start | bytes 294920 | tf_op jit(solution)/shard_map/ppermute | solution.py:263
  128.0 15.6 %collective-permute-start.13 = (bf16[64,768]{1,0:T(8,128)(2,1)S(1)}, bf16[64,768]{1,0:T(8,128)(2,1)S(1)}, u32[]{:S(2)}, u32[]{:S(2)}) collective-permute-start(bf16[64,768]{1,0:T(8,128)(2,1)S(1)} %get-tuple-element.34), channel_id=1, source_target_pairs={{0,20},{2,22},{4,16},{6,18},{8,28},{10,30},{12,24},{14,26},{16,4},... | collective-permute-start | bytes 294920 | tf_op jit(solution)/shard_map/ppermute | solution.py:263
  130.0 15.7 %collective-permute-start.14 = (bf16[64,768]{1,0:T(8,128)(2,1)S(1)}, bf16[64,768]{1,0:T(8,128)(2,1)S(1)}, u32[]{:S(2)}, u32[]{:S(2)}) collective-permute-start(bf16[64,768]{1,0:T(8,128)(2,1)S(1)} %get-tuple-element.35), channel_id=1, source_target_pairs={{0,22},{2,20},{4,18},{6,16},{8,30},{10,28},{12,26},{14,24},{16,6},... | collective-permute-start | bytes 294920 | tf_op jit(solution)/shard_map/ppermute | solution.py:263
  (31 other events, 115.1 us)
